TPU v7x, 32 devices: a whole 2x2x4 slice. The times are simulated.
32 devices in a mesh: ctx: 8 (over z, x), head: 4 (over y, core).
Axes of the slice: x: 2, y: 2, z: 4, core: 2. Of those that a mesh axis runs over, the one named last changes fastest.
Arguments:
- x_load: bfloat16 [4096, 8192], P('ctx', 'head'), may hold values from -6 to 6
- bc_load: bfloat16 [4096, 256], P('ctx'), may hold values from -0.59765625 to 0.59765625
- dt_load: bfloat16 [4096, 128], P('ctx', 'head'), may hold values from 0.34960938 to 2.796875
- decay_rate: float32 [128], P('head'), may hold values from 6.1035156e-05 to 0.02
- doc_ids: int32 [4096], P('ctx'), may hold values from 0 to 3, never falling along the last dimension, each value on 1 to 3072 neighbouring positions
- destination: int32 [4096], replicated, may hold values from 0 to 4095, as said below
- grad_y: bfloat16 [4096, 8192], P('ctx', 'head'), may hold values from -6 to 6
Outputs:
- scan_output: bfloat16 [4096, 8192], P('ctx', 'head')
- dx_load: bfloat16 [4096, 8192], P('ctx', 'head')
- dbc_load: bfloat16 [4096, 256], P('ctx')
- ddt_load: bfloat16 [4096, 128], P('ctx', 'head')
Inputs may be any that keep to these rules, and one draw needn't show every extreme that they name: `destination`: a permutation of the 4096 context positions; the rows of one loader device (aligned blocks of 512 rows) send at most 128 rows to the positions of one context device, and some pairs of devices reach 128. `doc_ids`: never falling along the positions; each document is 1 to 3072 positions long, one exactly 3072.
All inputs are finite; a program needn't handle non-finite values.
Results may differ from a plain program's by a relative error of at most 0.001.
Values may be sent and summed in bfloat16 or wider, within the bound.
No kernel may reach another device: no remote copies, remote signals or barrier semaphores. Data moves between devices by JAX's collectives and lax.ppermute only.
A program may use at most 192 MiB of HBM per device.

v0:
```python
import jax
import jax.numpy as jnp
from jax import lax
from jax.sharding import PartitionSpec as P

BLOCK = 256


PRECISE = lax.Precision.HIGHEST


def carried_in(part, axis, combine, identity, reverse):
    count = lax.axis_size(axis)
    place = lax.axis_index(axis)
    ahead = count - 1 - place if reverse else place
    gathered = jax.tree.map(lambda a: lax.all_gather(a, axis), part)
    state = jax.tree.map(lambda a, e: jnp.zeros_like(a) + jnp.asarray(e, a.dtype), part, identity)

    def one(step, state):
        source = count - 1 - step if reverse else step
        return combine(
            state, jax.tree.map(lambda a: lax.dynamic_index_in_dim(a, source, 0, False), gathered)
        )

    return lax.fori_loop(0, ahead, one, state)


def routing(destination, rows_dev, shards):
    owners = destination // rows_dev
    sources = jnp.arange(destination.shape[0], dtype=jnp.int32) // rows_dev
    onehot = (owners[:, None] == jnp.arange(shards, dtype=jnp.int32)[None, :]).astype(jnp.int32)
    blocks = onehot.reshape(shards, rows_dev, shards)
    before = jnp.cumsum(blocks, axis=1) - blocks
    rank_of = jnp.sum(before * blocks, axis=2).reshape(-1)
    return (owners, sources, rank_of)


def to_slots(values, my_slots, total_slots):
    return jnp.zeros((total_slots,) + values.shape[1:], values.dtype).at[my_slots].set(values)


def join_forward(earlier, follower):
    pass_a, states_a, head_a, tail_a = earlier
    pass_b, states_b, head_b, tail_b = follower
    linked = ((head_b == tail_a) | (tail_a < 0) | (head_b < 0)).astype(jnp.float32)
    joined = pass_b * linked
    return (
        pass_a * joined,
        joined[:, None, None] * states_a + states_b,
        jnp.where(head_a < 0, head_b, head_a),
        jnp.where(tail_b < 0, tail_a, tail_b),
    )


def join_backward(earlier, follower):
    pass_h, states_h, head_h, tail_h = earlier
    pass_l, states_l, head_l, tail_l = follower
    linked = ((head_h == tail_l) | (tail_l < 0) | (head_h < 0)).astype(jnp.float32)
    joined = pass_l * linked
    return (
        pass_h * joined,
        joined[:, None, None] * states_h + states_l,
        jnp.where(head_l < 0, head_h, head_l),
        jnp.where(tail_h < 0, tail_l, tail_h),
    )


def intra_block(pieces):
    running, doc_block, b_block, c_block, scaled, grad_out = pieces
    positions = jnp.arange(doc_block.shape[0], dtype=jnp.int32)
    same_doc = (doc_block[:, None] == doc_block[None, :]) & (
        positions[:, None] >= positions[None, :]
    )
    running_t = running.T
    log_gaps = running_t[:, :, None] - running_t[:, None, :]
    weights = jnp.where(same_doc[None], jnp.exp(jnp.where(same_doc[None], log_gaps, 0.0)), 0.0)
    affinity = jnp.dot(c_block, b_block.T, precision=PRECISE, preferred_element_type=jnp.float32)
    mixing = weights * affinity[None]
    y_local = jnp.einsum("hij,jhp->ihp", mixing, scaled, precision=PRECISE)
    pair_dots = jnp.einsum("ihp,jhp->hij", grad_out, scaled, precision=PRECISE)
    masked = pair_dots * weights
    dc_local = jnp.einsum("hij,jn->in", masked, b_block, precision=PRECISE)
    db_local = jnp.einsum("hij,in->jn", masked, c_block, precision=PRECISE)
    du_local = jnp.einsum("hij,ihp->jhp", mixing, grad_out, precision=PRECISE)
    return (y_local, du_local, dc_local, db_local)


def body(x_load, bc_load, dt_load, decay_rate, doc_ids, destination, grad_y):
    shards = lax.axis_size("ctx")
    myself = lax.axis_index("ctx")
    rows_dev = x_load.shape[0]
    capacity = 2 * rows_dev // shards
    total_slots = shards * capacity
    owners, sources, rank_of = routing(destination, rows_dev, shards)
    slot_all = owners * capacity + rank_of
    my_slots = lax.dynamic_slice_in_dim(slot_all, myself * rows_dev, rows_dev)
    arrive = jnp.where(owners == myself, destination % rows_dev, rows_dev)
    pick_rows = (
        jnp.zeros((rows_dev,), jnp.int32).at[arrive].set(sources * capacity + rank_of, mode="drop")
    )
    slot_back = jnp.where(owners == myself, sources * capacity + rank_of, total_slots)
    back_rows = (
        jnp.zeros((total_slots,), jnp.int32).at[slot_back].set(destination % rows_dev, mode="drop")
    )
    recv_x, recv_bc, recv_dt = (
        lax.all_to_all(
            to_slots(x_load, my_slots, total_slots), "ctx", split_axis=0, concat_axis=0, tiled=True
        ),
        lax.all_to_all(
            to_slots(bc_load, my_slots, total_slots), "ctx", split_axis=0, concat_axis=0, tiled=True
        ),
        lax.all_to_all(
            to_slots(dt_load, my_slots, total_slots), "ctx", split_axis=0, concat_axis=0, tiled=True
        ),
    )
    x_ctx = jnp.take(recv_x, pick_rows, axis=0)
    dt_ctx = jnp.take(recv_dt, pick_rows, axis=0)
    bc_part = jnp.take(recv_bc, pick_rows, axis=0)
    heads_dev = dt_load.shape[1]
    head_dim = x_load.shape[1] // heads_dev
    state_dim = bc_part.shape[1] // 2
    block_count = rows_dev // BLOCK
    x_float = x_ctx.astype(jnp.float32).reshape(block_count, BLOCK, heads_dev, head_dim)
    dt_float = dt_ctx.astype(jnp.float32).reshape(block_count, BLOCK, heads_dev)
    b_float = bc_part[:, :state_dim].astype(jnp.float32).reshape(block_count, BLOCK, state_dim)
    c_float = bc_part[:, state_dim:].astype(jnp.float32).reshape(block_count, BLOCK, state_dim)
    dy_float = grad_y.astype(jnp.float32).reshape(block_count, BLOCK, heads_dev, head_dim)
    doc_blocks = doc_ids.reshape(block_count, BLOCK)
    running = jnp.cumsum(-decay_rate[None, None, :] * dt_float, axis=1)
    totals = running[:, -1, :]
    scaled = dt_float[..., None] * x_float
    doc_last = doc_blocks[:, -1]
    doc_prev = jnp.concatenate([doc_blocks[:1, 0], doc_blocks[:-1, -1]])
    shard_first = doc_blocks[0, 0]
    shard_last = doc_blocks[-1, -1]
    enter_w = jnp.where((doc_blocks == doc_prev[:, None])[..., None], jnp.exp(running), 0.0)
    leave_w = jnp.where(
        (doc_blocks == doc_last[:, None])[..., None], jnp.exp(totals[:, None, :] - running), 0.0
    )
    carry_k = jnp.exp(totals) * (doc_last == doc_prev).astype(jnp.float32)[:, None]
    block_states = jnp.einsum("kjh,kjn,kjhp->khnp", leave_w, b_float, scaled, precision=PRECISE)
    back_states = jnp.einsum("kih,kin,kihp->khnp", enter_w, c_float, dy_float, precision=PRECISE)

    def forward_step(carried, pieces):
        factor, fresh_state = pieces
        return (factor[:, None, None] * carried + fresh_state, carried)

    def backward_step(carried, pieces):
        factor, fresh_state = pieces
        return (fresh_state + factor[:, None, None] * carried, carried)

    start_state = jnp.zeros((heads_dev, state_dim, head_dim), jnp.float32)
    local_exit, local_entry = lax.scan(forward_step, start_state, (carry_k, block_states))
    local_back, local_exit_grad = lax.scan(
        backward_step, start_state, (carry_k, back_states), reverse=True
    )
    pass_all = jnp.prod(carry_k, axis=0)
    unit_row = jnp.ones((1, heads_dev), jnp.float32)
    before_prod = jnp.concatenate([unit_row, jnp.cumprod(carry_k[:-1], axis=0)], axis=0)
    after_prod = jnp.concatenate([jnp.cumprod(carry_k[::-1], axis=0)[::-1][1:], unit_row], axis=0)
    first_tag = shard_first.astype(jnp.float32)
    last_tag = shard_last.astype(jnp.float32)
    identity = (
        jnp.ones((heads_dev,), jnp.float32),
        start_state,
        jnp.float32(-1.0),
        jnp.float32(-1.0),
    )
    _, state_in, _, tag_in = carried_in(
        (pass_all, local_exit, first_tag, last_tag), "ctx", join_forward, identity, False
    )
    _, grad_in, tag_out, _ = carried_in(
        (pass_all, local_back, first_tag, last_tag), "ctx", join_backward, identity, True
    )
    y_local, du_local, dc_local, db_local = lax.map(
        intra_block, (running, doc_blocks, b_float, c_float, scaled, dy_float)
    )
    state_kept = state_in * (tag_in == first_tag).astype(jnp.float32)
    grad_kept = grad_in * (tag_out == last_tag).astype(jnp.float32)
    entering = local_entry + before_prod[:, :, None, None] * state_kept[None]
    exit_grad = local_exit_grad + after_prod[:, :, None, None] * grad_kept[None]
    link_term = pass_all * jnp.sum(grad_kept * state_kept, axis=(1, 2))
    tail_term = jnp.sum(grad_kept * local_exit, axis=(1, 2))
    y_total = y_local + enter_w[..., None] * jnp.einsum(
        "kin,khnp->kihp", c_float, entering, precision=PRECISE
    )
    dc_total = dc_local + jnp.einsum(
        "kih,khnp,kihp->kin", enter_w, entering, dy_float, precision=PRECISE
    )
    du_total = du_local + leave_w[..., None] * jnp.einsum(
        "kjn,khnp->kjhp", b_float, exit_grad, precision=PRECISE
    )
    db_total = db_local + jnp.einsum(
        "kjh,khnp,kjhp->kjn", leave_w, exit_grad, scaled, precision=PRECISE
    )
    values = jnp.sum(dy_float * y_total, axis=-1) - jnp.sum(scaled * du_total, axis=-1)
    positions = jnp.arange(BLOCK, dtype=jnp.int32)

    def suffix_step(carry_pair, pieces):
        carried_sum, carried_tag = carry_pair
        doc_block, block_values = pieces
        later_mask = (doc_block[:, None] == doc_block[None, :]) & (
            positions[None, :] >= positions[:, None]
        )
        inside = jnp.dot(
            later_mask.astype(jnp.float32),
            block_values,
            precision=PRECISE,
            preferred_element_type=jnp.float32,
        )
        result = inside + jnp.where(
            (doc_block.astype(jnp.float32) == carried_tag)[:, None], carried_sum[None, :], 0.0
        )
        return ((result[0], doc_block[0].astype(jnp.float32)), result)

    _, suffix = lax.scan(
        suffix_step,
        (jnp.zeros((heads_dev,), jnp.float32), jnp.float32(-1.0)),
        (doc_blocks, values),
        reverse=True,
    )
    decay_grad = (
        suffix
        + jnp.where((doc_blocks == shard_last)[..., None], tail_term[None, None, :], 0.0)
        + link_term[None, None, :]
    )
    step_grad = jnp.sum(x_float * du_total, axis=-1) - decay_rate[None, None, :] * decay_grad
    input_grad = dt_float[..., None] * du_total
    scan_output = y_total.reshape(rows_dev, heads_dev * head_dim).astype(jnp.bfloat16)
    dx_ctx = input_grad.reshape(rows_dev, heads_dev * head_dim).astype(jnp.bfloat16)
    ddt_ctx = step_grad.reshape(rows_dev, heads_dev).astype(jnp.bfloat16)
    bc_partial = jnp.concatenate([db_total, dc_total], axis=-1).reshape(rows_dev, 2 * state_dim)
    bc_grad = lax.psum(bc_partial, "head").astype(jnp.bfloat16)
    back_dx, back_bc, back_dt = (
        lax.all_to_all(
            jnp.take(dx_ctx, back_rows, axis=0), "ctx", split_axis=0, concat_axis=0, tiled=True
        ),
        lax.all_to_all(
            jnp.take(bc_grad, back_rows, axis=0), "ctx", split_axis=0, concat_axis=0, tiled=True
        ),
        lax.all_to_all(
            jnp.take(ddt_ctx, back_rows, axis=0), "ctx", split_axis=0, concat_axis=0, tiled=True
        ),
    )
    dx_load = jnp.take(back_dx, my_slots, axis=0)
    ddt_load = jnp.take(back_dt, my_slots, axis=0)
    bc_rows_back = jnp.take(back_bc, my_slots, axis=0)
    return (scan_output, dx_load, bc_rows_back, ddt_load)


def solution(mesh):
    return jax.shard_map(
        body,
        mesh=mesh,
        in_specs=(
            P("ctx", "head"),
            P("ctx", None),
            P("ctx", "head"),
            P("head"),
            P("ctx"),
            P(),
            P("ctx", "head"),
        ),
        out_specs=(P("ctx", "head"), P("ctx", "head"), P("ctx", None), P("ctx", "head")),
        check_vma=False,
    )
```

profile of v0, /device:TPU:0, one launch (start us, length us, event | category | flops | bytes accessed | tf_op | source)
XLA Modules:
  0.0 787.4 jit_solution(6313097983738732914)
XLA Ops:
  7.9 9.0 %reduce-window.14 = s32[8,8,4,128]{3,1,2,0:T(8,128)S(1)} reduce-window(s32[8,8,4,128]{3,1,2,0:T(8,128)S(1)} %fusion.102, s32[]{:T(128)} %copy.216), window={size=1x1x1x128 pad=0_0x0_0x0_0x127_0}, to_apply=%region_0.1 | reduce-window | flops 4161536 | bytes 262148 | tf_op jit(solution)/shard_map/reduce-window
  21.7 7.3 all-to-all-start
  31.6 15.5 %scatter_custom_fusion.1 = s32[512]{0:T(512)S(1)} fusion(s32[4096]{0:T(1024)S(1)} %get-tuple-element.801, s32[4096]{0:T(1024)S(1)} %get-tuple-element.802, s32[]{:T(128)} %copy.216), kind=kCustom, calls=%fused_computation.200 | custom fusion | bytes 2052 | tf_op jit(solution)/shard_map/scatter | solution.py:99
  55.5 7.4 reshape.479
  62.9 7.8 copy.63
  72.2 6.0 all-to-all-start.2
  83.3 8.9 %all-to-all-done.2 = bf16[8,128,256]{2,1,0:T(8,128)(2,1)S(1)} async-done(((bf16[8,128,256]{2,1,0:T(8,128)(2,1)}), bf16[8,128,256]{2,1,0:T(8,128)(2,1)S(1)}, u32[]{:S(2)}, u32[]{:S(2)}) %all-to-all-start.2) | async-done | bytes 524320 | tf_op jit(solution)/shard_map/all_to_all | solution.py:109
  94.3 5.6 fusion.80
  102.3 14.2 %while.102 = (s32[]{:T(128)}, f32[32,128,64]{2,1,0:T(8,128)S(1)}, f32[2,32,128,64]{3,2,1,0:T(8,128)}, f32[2,32,128,64]{2,3,1,0:T(8,128)}, f32[2,32]{1,0:T(2,128)}, /*index=5*/s32[]{:T(128)}, s32[]{:T(128)}) while((s32[]{:T(128)}, f32[32,128,64]{2,1,0:T(8,128)S(1)}, f32[2,32,128,64]{3,2,1,0:T(8,128)}, ...), condition=%wide.region_20.24_spmd.clone, body=%wide.region_19.23_spmd.clone.sunk | while | flops 1048580 | bytes 18874900 | solution.py:154
  118.1 7.2 scatter_custom_fusion.2
  125.4 4.6 all-to-all-start.1
  130.5 179.7 %all-to-all-done.1 = bf16[8,128,2048]{2,1,0:T(8,128)(2,1)} async-done(((bf16[8,128,2048]{2,1,0:T(8,128)(2,1)}), bf16[8,128,2048]{2,1,0:T(8,128)(2,1)}, u32[]{:S(2)}, u32[]{:S(2)}) %all-to-all-start.1) | async-done | bytes 4194336 | tf_op jit(solution)/shard_map/all_to_all | solution.py:106
  310.3 8.0 %gather_fusion.4 = bf16[512,2048]{1,0:T(8,128)(2,1)} fusion(bf16[1024,2048]{1,0:T(8,128)(2,1)} %bitcast.30, s32[1024]{0:T(1024)S(1)} %pad_clamp_fusion.1), kind=kCustom, calls=%fused_computation.2.clone | custom fusion | bytes 4196352 | tf_op jit(solution)/shard_map/jit(_take)/gather | solution.py:116
  318.2 3.9 select_convert_fusion
  322.1 7.8 reshape.478
  330.0 7.8 copy.58
  337.8 5.7 fusion.77
  345.9 12.7 %while.101 = (s32[]{:T(128)}, f32[32,128,64]{2,1,0:T(8,128)S(1)}, f32[2,32,128,64]{3,2,1,0:T(8,128)}, f32[2,32]{1,0:T(2,128)S(1)}, f32[2,32,128,64]{2,3,1,0:T(8,128)}, /*index=5*/s32[]{:T(128)}, s32[]{:T(128)}) while((s32[]{:T(128)}, f32[32,128,64]{2,1,0:T(8,128)S(1)}, f32[2,32,128,64]{3,2,1,0:T(8,128)}, ...), condition=%wide.region_13.17_spmd.clone, body=%wide.region_12.16_spmd.clone.sunk | while | flops 1048579 | bytes 18874888 | solution.py:153
  364.4 15.6 %scatter_custom_fusion.4 = s32[1024]{0:T(1024)S(1)} fusion(s32[4096]{0:T(1024)} %get-tuple-element.788, s32[4096]{0:T(1024)} %get-tuple-element.800, s32[]{:T(128)} %copy.216), kind=kCustom, calls=%fused_computation.189 | custom fusion | bytes 4608 | tf_op jit(solution)/shard_map/scatter | solution.py:103
  380.4 19.3 %all-reduce.4 = (f32[256]{0:T(256)S(1)}, f32[8]{0:T(128)S(1)}, f32[8]{0:T(128)S(1)}) all-reduce(f32[256]{0:T(256)S(1)} %dynamic-update-slice, f32[8]{0:T(128)S(1)} %bitcast_dynamic-update-slice_fusion.5, f32[8]{0:T(128)S(1)} %dynamic-update-slice.2), channel_id=2, replica_groups=mesh['ctx'=8,'head'=4] {'ctx'}, use_global_device_ids=true, to_apply=%add.1 | all-reduce | flops 272 | bytes 2176
  399.9 5.2 broadcast_multiply_fusion
  405.1 62.0 %while.97 = (s32[]{:T(128)}, f32[2,256,32,64]{1,3,2,0:T(8,128)}, f32[2,256,32,64]{1,3,2,0:T(8,128)}, f32[2,256,128]{1,2,0:T(8,128)S(1)}, f32[2,256,128]{1,2,0:T(...) while((s32[]{:T(128)}, f32[2,256,32,64]{1,3,2,0:T(8,128)}, ...), condition=%wide.region_11.15_spmd, body=%wide.region_9.14_spmd.sunk | while | flops 5161222144 | bytes 84682032 | solution.py:175
  405.8 11.9 %bitcast_dynamic-update-slice_fusion.11 = f32[2,256,32,64]{1,3,2,0:T(8,128)} fusion(f32[2,256,32,64]{1,3,2,0:T(8,128)} %get-tuple-element.1094, s32[]{:T(128)S(6)} %copy.148, f32[256,256]{1,0:T(8,128)S(1)} %fusion.167, f32[32,256]{1,0:T(8,128)S(1)} %dynamic-slice_bitcast_fusion.2, pred[256,256]{1,0:T(8,128)(4,1)S(1)} %fusion.168, ...), kind=kOutput, calls=%fused_computation.31.clone.1 | convolution fusion | flops 1619001344 | bytes 4588544 | tf_op jit(solution)/shard_map/while/body/eval_jaxpr/hij,jhp->ihp/dot_general | solution.py:79
  417.8 7.1 bitcast_dynamic-update-slice_fusion.12
  424.9 9.6 %multiply_reduce_fusion.7 = f32[256,256]{1,0:T(8,128)S(1)} fusion(f32[32,256]{1,0:T(8,128)S(1)} %dynamic-slice_bitcast_fusion.2, pred[256,256]{1,0:T(8,128)(4,1)S(1)} %fusion.168, f32[2,256,32,64]{1,3,2,0:T(8,128)S(1)} %copy-done.1, s32[]{:T(128)S(6)} %copy.148, f32[2,256,32,64]{1,3,2,0:T(8,128)S(1)} %copy-done.12), kind=kOutput, calls=%fused_computation.15.clone.1 | convolution fusion | flops 1621032960 | bytes 4588544 | tf_op jit(solution)/shard_map/while/body/eval_jaxpr/ihp,jhp->hij/dot_general | solution.py:80
  436.6 11.9 %bitcast_dynamic-update-slice_fusion.11 = f32[2,256,32,64]{1,3,2,0:T(8,128)} fusion(f32[2,256,32,64]{1,3,2,0:T(8,128)} %get-tuple-element.1094, s32[]{:T(128)S(6)} %copy.148, f32[256,256]{1,0:T(8,128)S(1)} %fusion.167, f32[32,256]{1,0:T(8,128)S(1)} %dynamic-slice_bitcast_fusion.2, pred[256,256]{1,0:T(8,128)(4,1)S(1)} %fusion.168, ...), kind=kOutput, calls=%fused_computation.31.clone.1 | convolution fusion | flops 1619001344 | bytes 4588544 | tf_op jit(solution)/shard_map/while/body/eval_jaxpr/hij,jhp->ihp/dot_general | solution.py:79
  448.5 7.1 bitcast_dynamic-update-slice_fusion.12
  455.6 9.6 %multiply_reduce_fusion.7 = f32[256,256]{1,0:T(8,128)S(1)} fusion(f32[32,256]{1,0:T(8,128)S(1)} %dynamic-slice_bitcast_fusion.2, pred[256,256]{1,0:T(8,128)(4,1)S(1)} %fusion.168, f32[2,256,32,64]{1,3,2,0:T(8,128)S(1)} %copy-done.1, s32[]{:T(128)S(6)} %copy.148, f32[2,256,32,64]{1,3,2,0:T(8,128)S(1)} %copy-done.12), kind=kOutput, calls=%fused_computation.15.clone.1 | convolution fusion | flops 1621032960 | bytes 4588544 | tf_op jit(solution)/shard_map/while/body/eval_jaxpr/ihp,jhp->hij/dot_general | solution.py:80
  468.8 76.0 %while.99 = (s32[]{:T(128)}, f32[32,128,64]{2,1,0:T(8,128)}, f32[]{:T(128)}, s32[]{:T(128)}, f32[8,32]{1,0:T(8,128)S(1)}, /*index=5*/f32[8]{0:T(128)S(1)}, f32[8...) while((s32[]{:T(128)}, f32[32,128,64]{2,1,0:T(8,128)}, ...), condition=%wide.region_23.27_spmd, body=%wide.region_22.26_spmd.sunk | while | flops 524334 | bytes 7340691 | solution.py:25
  473.9 3.8 bitcast_add_fusion.9
  495.6 3.8 bitcast_add_fusion.9
  546.3 4.3 multiply_reduce_fusion.5
  568.6 6.1 fusion.90
  574.8 4.3 fusion.93
  579.4 16.6 %all-reduce.6 = bf16[512,256]{1,0:T(8,128)(2,1)S(1)} all-reduce(f32[512,256]{1,0:T(8,128)S(1)} %bitcast.280), channel_id=1, replica_groups=mesh['ctx'=8,'head'=4] {'head'}, use_global_device_ids=true, to_apply=%region_24.28 | all-reduce | flops 131072 | bytes 786432 | tf_op jit(solution)/shard_map/psum | solution.py:233
  596.0 13.1 %multiply_reduce_fusion.1 = (f32[2,256,32]{1,2,0:T(8,128)S(1)}, f32[2,256,32]{1,2,0:T(8,128)S(1)}, f32[2,256,32,64]{1,3,2,0:T(8,128)}, bf16[2,256,32,64]{1,3,2,0:T(8,128)(2,1)}, f32[2,256,32]{1,2,0:T(8,128)S(1)}) fusion(f32[2,256,32,64]{1,3,2,0:T(8,128)} %copy.58, f32[2,256,32,64]{1,3,2,0:T(8,128)} %get-tuple-element.546, f32[2,256,32]{1,2,0:T(8,128)S(1)} %copy-done.16, ...), kind=kLoop, calls=%fused_computation.95 | loop fusion | flops 12533760 | bytes 31850496 | tf_op jit(solution)/shard_map/reduce_sum | solution.py:196
  612.8 3.9 gather_fusion.1
  620.7 17.5 %all-to-all-start.5 = ((bf16[8,128,32]{1,2,0:T(8,128)(2,1)}), bf16[8,128,32]{1,2,0:T(8,128)(2,1)S(1)}, u32[]{:S(2)}, u32[]{:S(2)}) async-start(bf16[8,128,32]{1,2,0:T(8,128)(2,1)} %broadcast_select_fusion.7), calls=%async_computation.5 | async-start | bytes 131072 | tf_op jit(solution)/shard_map/all_to_all | solution.py:241
  639.2 5.9 all-to-all-done.5
  651.4 6.6 copy.96
  658.0 5.8 reshape.477
  663.8 6.0 gather_fusion
  669.8 4.6 broadcast_select_fusion
  674.4 6.3 all-to-all-start.3
  680.8 6.6 copy.95
  687.4 6.7 reshape.476
  699.3 72.3 %all-to-all-done.3 = bf16[8,128,2048]{2,1,0:T(8,128)(2,1)} async-done(((bf16[8,128,2048]{2,1,0:T(8,128)(2,1)}), bf16[8,128,2048]{2,1,0:T(8,128)(2,1)}, u32[]{:S(2)}, u32[]{:S(2)}) %all-to-all-start.3) | async-done | bytes 4194336 | tf_op jit(solution)/shard_map/all_to_all | solution.py:235
  771.6 7.1 gather_fusion.6
  (274 shorter events, 162.0 us)
Async XLA Ops:
  19.1 99.0 %copy-start.25 = (s32[512]{0:T(512)}, s32[512]{0:T(512)S(1)}, u32[]{:S(2)}) copy-start(s32[512]{0:T(512)S(1)} %get-tuple-element.787) | copy-start | bytes 6148
  21.7 50.5 %all-to-all-start = ((bf16[8,128,32]{1,2,0:T(8,128)(2,1)}), bf16[8,128,32]{1,2,0:T(8,128)(2,1)S(1)}, u32[]{:S(2)}, u32[]{:S(2)}) async-start(bf16[8,128,32]{1,2,0:T(8,128)(2,1)} %copy.54), calls=%async_computation | async-start | bytes 131072 | tf_op jit(solution)/shard_map/all_to_all | solution.py:112
  72.2 20.0 %all-to-all-start.2 = ((bf16[8,128,256]{2,1,0:T(8,128)(2,1)}), bf16[8,128,256]{2,1,0:T(8,128)(2,1)S(1)}, u32[]{:S(2)}, u32[]{:S(2)}) async-start(bf16[8,128,256]{2,1,0:T(8,128)(2,1)} %bitcast.34), calls=%async_computation.2 | async-start | bytes 1048576 | tf_op jit(solution)/shard_map/all_to_all | solution.py:109
  78.2 389.0 %all-gather.9.cloned.1.call-start = ((), (), s32[]{:S(2)}) async-start(), calls=%async_computation.7 | async-start | bytes 9437184 | tf_op jit(solution)/shard_map/all_gather | solution.py:16
  81.8 1.4 copy-start.17
  83.2 16.6 %copy-start.13 = (f32[2,256,32]{1,2,0:T(8,128)}, f32[2,256,32]{1,2,0:T(8,128)S(1)}, u32[]{:S(2)}) copy-start(f32[2,256,32]{1,2,0:T(8,128)S(1)} %get-tuple-element.798) | copy-start | bytes 196612
  83.2 254.5 %copy-start.15 = (f32[2,256,32]{1,2,0:T(8,128)}, f32[2,256,32]{1,2,0:T(8,128)S(1)}, u32[]{:S(2)}) copy-start(f32[2,256,32]{1,2,0:T(8,128)S(1)} %get-tuple-element.799) | copy-start | bytes 196612
  102.3 2.3 copy-start.4
  109.4 2.4 copy-start.4
  125.4 184.9 %all-to-all-start.1 = ((bf16[8,128,2048]{2,1,0:T(8,128)(2,1)}), bf16[8,128,2048]{2,1,0:T(8,128)(2,1)}, u32[]{:S(2)}, u32[]{:S(2)}) async-start(bf16[8,128,2048]{2,1,0:T(8,128)(2,1)} %bitcast.265), calls=%async_computation.1 | async-start | bytes 8388608 | tf_op jit(solution)/shard_map/all_to_all | solution.py:106
  130.0 414.8 %all-gather.7.cloned.1.call-start = ((), (), s32[]{:S(2)}) async-start(), calls=%async_computation.6 | async-start | bytes 9437184 | tf_op jit(solution)/shard_map/all_gather | solution.py:16
  337.8 8.2 %copy-start.27 = (f32[2,32]{1,0:T(2,128)S(1)}, f32[2,32]{1,0:T(2,128)}, u32[]{:S(2)}) copy-start(f32[2,32]{1,0:T(2,128)} %get-tuple-element.1274) | copy-start | bytes 772
  345.9 2.3 copy-start.5
  352.3 2.4 copy-start.5
  358.7 3.0 copy-start.32
  358.7 21.4 %copy-start.31 = (f32[32]{0:T(128)S(1)}, f32[32]{0:T(128)}, u32[]{:S(2)}) copy-start(f32[32]{0:T(128)} %get-tuple-element.790) | copy-start | bytes 388
  358.7 41.1 %copy-start.30 = (pred[2]{0:T(512)(128)(4,1)S(1)}, pred[2]{0:T(512)(128)(4,1)}, u32[]{:S(2)}) copy-start(pred[2]{0:T(512)(128)(4,1)} %constant.339.clone.1) | copy-start | bytes 10
  399.9 5.2 copy-start.18
  405.8 12.0 %copy-start.1 = (f32[2,256,32,64]{1,3,2,0:T(8,128)S(1)}, f32[2,256,32,64]{1,3,2,0:T(8,128)}, u32[]{:S(2)}) copy-start(f32[2,256,32,64]{1,3,2,0:T(8,128)} %get-tuple-element.1115) | copy-start | bytes 12582916 | tf_op jit(solution)/shard_map/while
  405.8 11.9 %copy-start.10 = (f32[2,256,32,64]{1,3,2,0:T(8,128)S(1)}, f32[2,256,32,64]{1,3,2,0:T(8,128)}, u32[]{:S(2)}) copy-start(f32[2,256,32,64]{1,3,2,0:T(8,128)} %get-tuple-element.1095) | copy-start | bytes 12582916 | tf_op jit(solution)/shard_map/while
  417.8 7.1 copy-start.12
  424.8 9.6 %copy-start.11 = (f32[2,256,32,64]{1,3,2,0:T(8,128)}, f32[2,256,32,64]{1,3,2,0:T(8,128)S(1)}, u32[]{:S(2)}) copy-start(f32[2,256,32,64]{1,3,2,0:T(8,128)S(1)} %bitcast_dynamic-update-slice_fusion.12) | copy-start | bytes 12582916 | tf_op jit(solution)/shard_map/while
  424.9 10.1 %copy-start.21 = (f32[2,256,128]{1,2,0:T(8,128)S(1)}, f32[2,256,128]{1,2,0:T(8,128)}, u32[]{:S(2)}) copy-start(f32[2,256,128]{1,2,0:T(8,128)} %get-tuple-element.1097) | copy-start | bytes 786436 | tf_op jit(solution)/shard_map/while
  435.3 0.7 copy-start.22
  436.6 11.9 %copy-start.1 = (f32[2,256,32,64]{1,3,2,0:T(8,128)S(1)}, f32[2,256,32,64]{1,3,2,0:T(8,128)}, u32[]{:S(2)}) copy-start(f32[2,256,32,64]{1,3,2,0:T(8,128)} %get-tuple-element.1115) | copy-start | bytes 12582916 | tf_op jit(solution)/shard_map/while
  436.6 11.9 %copy-start.10 = (f32[2,256,32,64]{1,3,2,0:T(8,128)S(1)}, f32[2,256,32,64]{1,3,2,0:T(8,128)}, u32[]{:S(2)}) copy-start(f32[2,256,32,64]{1,3,2,0:T(8,128)} %get-tuple-element.1095) | copy-start | bytes 12582916 | tf_op jit(solution)/shard_map/while
  448.5 7.1 copy-start.12
  455.6 9.6 %copy-start.11 = (f32[2,256,32,64]{1,3,2,0:T(8,128)}, f32[2,256,32,64]{1,3,2,0:T(8,128)S(1)}, u32[]{:S(2)}) copy-start(f32[2,256,32,64]{1,3,2,0:T(8,128)S(1)} %bitcast_dynamic-update-slice_fusion.12) | copy-start | bytes 12582916 | tf_op jit(solution)/shard_map/while
  455.6 10.1 %copy-start.21 = (f32[2,256,128]{1,2,0:T(8,128)S(1)}, f32[2,256,128]{1,2,0:T(8,128)}, u32[]{:S(2)}) copy-start(f32[2,256,128]{1,2,0:T(8,128)} %get-tuple-element.1097) | copy-start | bytes 786436 | tf_op jit(solution)/shard_map/while
  467.2 1.6 copy-start.19
  546.3 4.3 copy-start.7
  555.8 3.7 copy-start.6
  555.9 3.7 copy-start.8
  564.8 3.8 copy-start.2
  564.8 3.8 copy-start.14
  564.8 3.8 copy-start.20
  568.6 6.1 copy-start
  568.6 6.1 copy-start.3
  568.6 6.1 copy-start.16
  568.6 6.1 copy-start.23
  595.9 16.6 %copy-start.28 = (pred[2,256]{1,0:T(4,128)(4,1)S(1)}, pred[2,256]{1,0:T(4,128)(4,1)}, u32[]{:S(2)}) copy-start(pred[2,256]{1,0:T(4,128)(4,1)} %get-tuple-element.803) | copy-start | bytes 1540
  595.9 16.6 %copy-start.29 = (f32[32]{0:T(128)S(1)}, f32[32]{0:T(128)}, u32[]{:S(2)}) copy-start(f32[32]{0:T(128)} %param.28) | copy-start | bytes 388
  620.7 24.4 %all-to-all-start.5 = ((bf16[8,128,32]{1,2,0:T(8,128)(2,1)}), bf16[8,128,32]{1,2,0:T(8,128)(2,1)S(1)}, u32[]{:S(2)}, u32[]{:S(2)}) async-start(bf16[8,128,32]{1,2,0:T(8,128)(2,1)} %broadcast_select_fusion.7), calls=%async_computation.5 | async-start | bytes 131072 | tf_op jit(solution)/shard_map/all_to_all | solution.py:241
  645.1 29.3 %all-to-all-start.4 = ((bf16[8,128,256]{2,1,0:T(8,128)(2,1)}), bf16[8,128,256]{2,1,0:T(8,128)(2,1)S(1)}, u32[]{:S(2)}, u32[]{:S(2)}) async-start(bf16[8,128,256]{2,1,0:T(8,128)(2,1)} %broadcast_select_fusion.2), calls=%async_computation.4 | async-start | bytes 1048576 | tf_op jit(solution)/shard_map/all_to_all | solution.py:238
  674.4 6.4 copy-start.26
  674.4 6.4 copy-start.9
  674.4 97.2 %all-to-all-start.3 = ((bf16[8,128,2048]{2,1,0:T(8,128)(2,1)}), bf16[8,128,2048]{2,1,0:T(8,128)(2,1)}, u32[]{:S(2)}, u32[]{:S(2)}) async-start(bf16[8,128,2048]{2,1,0:T(8,128)(2,1)} %broadcast_select_fusion), calls=%async_computation.3 | async-start | bytes 8388608 | tf_op jit(solution)/shard_map/all_to_all | solution.py:235
  687.4 8.3 %copy-start.24 = (pred[512]{0:T(512)(128)(4,1)S(1)}, pred[512]{0:T(512)(128)(4,1)}, u32[]{:S(2)}) copy-start(pred[512]{0:T(512)(128)(4,1)} %get-tuple-element.786) | copy-start | bytes 1540
  (1 other events, 0.7 us)
Sparse Core Ops, SparseCore 0:
  118.2 203.9 all-gather.8
  360.5 122.4 all-gather.6
where the time goes:
time: 796 us; the launch traced here: 787 us
  waiting for transfers between devices  267 us (34%)
  local copies, waits for them, and re-layouts  206 us (26%)
  other arithmetic  106 us (13%)
  matrix products  89.5 us (11%)
  starting transfers between devices  46 us (6%)
  blocking collectives  35.8 us (4%)
  loops' own time  20.7 us (3%)
  between operations  17.1 us (2%)
    all_to_all x1, waiting for transfers between devices, body(): lax.all_to_all(to_slots(x_load, my_slots, total_slots), 'ctx', split_axis...  180 us
    all_to_all x1, waiting for transfers between devices, body(): lax.all_to_all(jnp.take(dx_ctx, back_rows, axis=0), 'ctx', split_axis=0,...  72.3 us
    dynamic_slice x28, local copies, waits for them, and re-layouts, one(): lax.dynamic_index_in_dim(a, source, 0, False)  30.7 us
    add x7, other arithmetic, join_backward(): joined[:, None, None] * states_h + states_l  26.7 us
    dot_general x2, matrix products, intra_block(): y_local = jnp.einsum('hij,jhp->ihp', mixing, scaled, precision=PRECISE)  23.9 us
    unnamed x1, blocking collectives  19.3 us
    dot_general x2, matrix products, intra_block(): pair_dots = jnp.einsum('ihp,jhp->hij', grad_out, scaled, precision=PRECISE)  19.2 us
    another operation x2, loops' own time, carried_in(): return lax.fori_loop(0, ahead, one, state)  18.5 us
  transfers between devices with their start and end apart: 8, of which 4 were waited for; matrix products, arithmetic and copies ran while one was open for 37% of the time, Pallas kernels for 0%

commit v1 on v0

v1 whole, which is shorter than its diff:
```python
import functools
import jax
import jax.numpy as jnp
from jax import lax
from jax.experimental import pallas as pl
from jax.experimental.pallas import tpu as pltpu
from jax.sharding import PartitionSpec as P

BLOCK = 256
F32, BF16, I32 = jnp.float32, jnp.bfloat16, jnp.int32
NN, NT, TN = (((1,), (0,)), ((), ())), (((1,), (1,)), ((), ())), (((0,), (0,)), ((), ()))
VMEM = pl.BlockSpec(memory_space=pltpu.VMEM)
SMEM = pl.BlockSpec(memory_space=pltpu.SMEM)


def dot(a, b, dims=NN):
    return lax.dot_general(a, b, dims, preferred_element_type=F32)


def split2(v):
    hi = v.astype(BF16)
    return hi, (v - hi.astype(F32)).astype(BF16)


def dot2(a, b, dims=NN):
    if isinstance(a, tuple):
        return dot(a[0], b, dims) + dot(a[1], b, dims)
    return dot(a, b[0], dims) + dot(a, b[1], dims)


def dot3(a, b, dims=NN):
    return dot(a[0], b[0], dims) + (dot(a[0], b[1], dims) + dot(a[1], b[0], dims))


def column(row):
    return jnp.broadcast_to(row.astype(F32), (128, row.shape[1])).T[:, :1]


def expander(heads, width, head_dim):
    h = lax.broadcasted_iota(I32, (heads, width), 0)
    c = lax.broadcasted_iota(I32, (heads, width), 1)
    return jnp.where(c // head_dim == h, 1.0, 0.0).astype(BF16)


def place_kernel(pieces, head_dim, dest_ref, dt_ref, *refs):
    bc_refs, (bc_out, dt_out) = refs[:pieces], refs[pieces:]
    size = bc_refs[0].shape[0]
    first = pl.program_id(0) * BLOCK
    acc_bc = jnp.zeros((BLOCK, bc_out.shape[1]), F32)
    acc_dt = jnp.zeros((BLOCK, dt_ref.shape[0]), F32)
    for e in range(pieces):
        here = lax.broadcasted_iota(I32, (BLOCK, size), 0) + first
        pick = jnp.where(here == dest_ref[:, e * size : (e + 1) * size], 1.0, 0.0).astype(BF16)
        acc_bc = acc_bc + dot(pick, bc_refs[e][...])
        acc_dt = acc_dt + dot(pick, dt_ref[:, e * size : (e + 1) * size], NT)
    bc_out[...] = acc_bc.astype(BF16)
    spread = expander(dt_ref.shape[0], dt_out.shape[1], head_dim)
    dt_out[...] = dot(acc_dt.astype(BF16), spread).astype(BF16)


def decays(dt_ref, rate_ref):
    rows = lax.broadcasted_iota(I32, (BLOCK, BLOCK), 0)
    cols = lax.broadcasted_iota(I32, (BLOCK, BLOCK), 1)
    lower = jnp.where(rows >= cols, 1.0, 0.0).astype(BF16)
    running = rate_ref[...] * dot(lower, dt_ref[...])
    return jnp.exp(-running), jnp.exp(running), jnp.exp(-running[BLOCK - 1 :, :])


def doc_state(doc_smem, block):
    last = doc_smem[block * BLOCK + BLOCK - 1]
    prev = jnp.where(block == 0, -1.0, doc_smem[jnp.maximum(block * BLOCK - 1, 0)])
    return prev, last


def back_kernel(
    blocks, doc_smem, doc_ref, dest_ref, rate_ref, bc_ref, dt_ref, dy_ref,
    du_out, grad_out, dx_out, grad_ref, dx_ref,
):
    step = pl.program_id(0)

    @pl.when(step == 0)
    def _():
        grad_ref[...] = jnp.zeros_like(grad_ref)

    @pl.when(step < blocks)
    def _():
        block = blocks - 1 - step
        b, c = bc_ref[:, :128], bc_ref[:, 128:]
        enter, leave, total = decays(dt_ref, rate_ref)
        prev, last = doc_state(doc_smem, block)
        row = doc_ref[...]
        col = column(row)
        rows = lax.broadcasted_iota(I32, (BLOCK, BLOCK), 0)
        cols = lax.broadcasted_iota(I32, (BLOCK, BLOCK), 1)
        later = (col == row) & (cols >= rows)
        affinity = split2(jnp.where(later, dot(b, c, NT), 0.0))
        dy = split2(enter * dy_ref[...].astype(F32))
        grad = grad_ref[...]
        grad_out[0] = grad
        carried = total * grad
        b_last = jnp.where(col == last, b.astype(F32), 0.0).astype(BF16)
        c_first = jnp.where(col == prev, c.astype(F32), 0.0).astype(BF16)
        du = leave * (dot3(affinity, dy) + dot2(b_last, split2(carried)))
        du_out[...] = du
        dx_ref[pl.ds(pl.multiple_of(block * BLOCK, BLOCK), BLOCK), :] = (
            dt_ref[...].astype(F32) * du
        ).astype(BF16)
        grad_ref[...] = jnp.where(prev == last, carried, 0.0) + dot2(c_first, dy, TN)

    @pl.when(step >= blocks)
    def _():
        want = column(dest_ref[...]).astype(I32)
        tokens = dx_ref.shape[0]
        here = lax.broadcasted_iota(I32, (BLOCK, tokens), 1)
        pick = jnp.where(here == want, 1.0, 0.0).astype(BF16)
        dx_out[...] = dot(pick, dx_ref[...]).astype(BF16)


def front_kernel(
    blocks, head_dim, doc_smem, dest_smem, doc_ref, dest_ref, x_ref, rate_ref, rate_col,
    bc_ref, dt_ref, dy_ref, du_ref, grad_ref,
    y_out, dbc_out, ddt_out, state_ref, sum_ref, dbc_ref, ddt_ref,
):
    step = pl.program_id(0)

    @pl.when(step == 0)
    def _():
        state_ref[...] = jnp.zeros_like(state_ref)
        sum_ref[...] = jnp.zeros_like(sum_ref)

    @pl.when(step < blocks)
    def _():
        block = step
        tokens, width = x_ref.shape
        here = lax.broadcasted_iota(I32, (BLOCK, tokens), 0) + block * BLOCK
        pick = jnp.where(here == dest_ref[...], 1.0, 0.0).astype(BF16)
        x = dot(pick, x_ref[...])
        b, c = bc_ref[:, :128], bc_ref[:, 128:]
        enter, leave, total = decays(dt_ref, rate_ref)
        prev, last = doc_state(doc_smem, block)
        row = doc_ref[...]
        col = column(row)
        rows = lax.broadcasted_iota(I32, (BLOCK, BLOCK), 0)
        cols = lax.broadcasted_iota(I32, (BLOCK, BLOCK), 1)
        same = col == row
        earlier = same & (rows >= cols)
        affinity = split2(jnp.where(earlier, dot(c, b, NT), 0.0))
        dy_now = dy_ref[...].astype(F32)
        dy = split2(enter * dy_now)
        scaled = dt_ref[...].astype(F32) * x
        ux = split2(leave * scaled)
        is_last, is_first = col == last, col == prev
        b_last = jnp.where(is_last, b.astype(F32), 0.0).astype(BF16)
        c_first = jnp.where(is_first, c.astype(F32), 0.0).astype(BF16)
        state = state_ref[...]
        state2 = split2(state)
        y = enter * (dot3(affinity, ux) + dot2(c_first, state2))
        y_out[...] = y.astype(BF16)
        state_ref[...] = total * (jnp.where(prev == last, state, 0.0) + dot2(b_last, ux, TN))
        pairs = split2(jnp.where(earlier, dot3(dy, ux, NT), 0.0))
        grad2 = split2(total * grad_ref[0])
        dc = dot2(pairs, b) + jnp.where(is_first, dot3(dy, state2, NT), 0.0)
        db = dot2(pairs, c, TN) + jnp.where(is_last, dot3(ux, grad2, NT), 0.0)
        here_rows = pl.ds(pl.multiple_of(block * BLOCK, BLOCK), BLOCK)
        dbc_ref[here_rows, :128] = db
        dbc_ref[here_rows, 128:] = dc
        du = du_ref[...]
        heads = sum_ref.shape[0]
        spread = expander(heads, width, head_dim)

        def by_head(v):
            hi, low = split2(v)
            rest = (v - hi.astype(F32) - low.astype(F32)).astype(BF16)
            return dot(spread, hi, NT) + dot(spread, low, NT) + dot(spread, rest, NT)

        balance = by_head(scaled * du - dy_now * y)
        hi, low = split2(balance)
        rest = (balance - hi.astype(F32) - low.astype(F32)).astype(BF16)
        before = jnp.where(same & (rows < cols), 1.0, 0.0).astype(BF16)
        prefix = dot(hi, before) + dot(low, before) + dot(rest, before)
        prefix = prefix + jnp.where(row == prev, sum_ref[:, :1], 0.0)
        sum_ref[...] = jnp.broadcast_to(
            prefix[:, BLOCK - 1 :] + balance[:, BLOCK - 1 :], sum_ref.shape
        )
        ddt = by_head(x * du) - rate_col[...] * prefix
        ddt = jnp.concatenate([ddt, jnp.zeros((128 - heads, BLOCK), F32)], axis=0)
        ddt_ref[here_rows, :] = ddt.T

    @pl.when(step >= blocks)
    def _():
        base = (step - blocks) * BLOCK

        def rows8(i, carry):
            at = pl.multiple_of(i * 8, 8)
            spots = [dest_smem[base + at + j] for j in range(8)]
            dbc_out[pl.ds(at, 8), :] = jnp.concatenate(
                [dbc_ref[pl.ds(s, 1), :] for s in spots], axis=0
            )
            small[pl.ds(at, 8), :] = jnp.concatenate(
                [ddt_ref[pl.ds(s, 1), :] for s in spots], axis=0
            )
            return carry

        def run(buffer):
            nonlocal small
            small = buffer
            lax.fori_loop(0, BLOCK // 8, rows8, 0, unroll=4)
            ddt_out[...] = buffer[...].T[: ddt_out.shape[0], :]

        small = None
        pl.run_scoped(run, pltpu.VMEM((BLOCK, 128), F32))


def params(**extra):
    return pltpu.CompilerParams(
        dimension_semantics=("arbitrary",), vmem_limit_bytes=60 << 20, **extra
    )


def body(x_load, bc_load, dt_load, decay_rate, doc_ids, destination, grad_y):
    shards, teams = lax.axis_size("ctx"), lax.axis_size("head")
    me, team = lax.axis_index("ctx"), lax.axis_index("head")
    rows_dev, chan_dev = x_load.shape
    heads_dev = dt_load.shape[1]
    head_dim = chan_dev // heads_dev
    width = chan_dev // shards
    tokens = rows_dev * shards
    blocks = tokens // BLOCK
    heads = max(1, width // head_dim)
    sharing = shards * heads // heads_dev
    padded = -(-heads // 8) * 8
    quarter = rows_dev // teams

    def exchange(v):
        return lax.all_to_all(v, "ctx", split_axis=0, concat_axis=0, tiled=True)

    def by_channel(v):
        parts = v.reshape(rows_dev, shards, width).transpose(1, 0, 2)
        return exchange(parts.reshape(tokens, width))

    own_bc = lax.dynamic_slice_in_dim(bc_load, team * quarter, quarter)
    sent_bc = jnp.broadcast_to(own_bc[None], (shards,) + own_bc.shape)
    part_bc = exchange(sent_bc.reshape(shards * quarter, -1))
    head_of = jnp.asarray([[k * width // head_dim + h for h in range(heads)] for k in range(shards)])
    dt_rows = dt_load.T[head_of]
    doc_rows = jnp.broadcast_to(doc_ids.astype(BF16)[None, None], (shards, 1, rows_dev))
    small = exchange(jnp.concatenate([dt_rows, doc_rows], axis=1).reshape(-1, rows_dev))
    small = small.reshape(shards, heads + 1, rows_dev)
    docs = small[:, heads].astype(F32).reshape(tokens)
    dt_all = small[:, :heads].transpose(1, 0, 2).reshape(heads, tokens)
    pieces = [part_bc]
    for e in range(1, teams):
        pieces.append(lax.ppermute(part_bc, "head", [(i, i ^ e) for i in range(teams)]))
    order = jnp.stack([team ^ e for e in range(teams)])
    dest_bc = jnp.take(destination.reshape(shards, teams, quarter), order, axis=1)
    dest_bc = dest_bc.transpose(1, 0, 2).reshape(1, tokens)
    dt_bc = jnp.take(dt_all.reshape(heads, shards, teams, quarter), order, axis=2)
    dt_bc = dt_bc.transpose(0, 2, 1, 3).reshape(heads, tokens)
    dt_bc = jnp.concatenate([dt_bc, jnp.zeros((16 - heads, tokens), BF16)], axis=0)

    dy_all = by_channel(grad_y)
    x_all = by_channel(x_load)

    rate_here = lax.dynamic_slice_in_dim(decay_rate, me * width // head_dim, heads)
    rate_row = jnp.repeat(rate_here, width // heads)[None]
    rate_col = jnp.concatenate([rate_here, jnp.zeros((padded - heads,), F32)])[:, None]
    dest_row, doc_row = destination[None], docs[None]

    def blocked(cols, index):
        return pl.BlockSpec((BLOCK, cols), lambda s: (index(s), 0))

    def rowed(rows, index):
        return pl.BlockSpec((rows, BLOCK), lambda s: (0, index(s)))

    bc_ctx, dt_ctx = pl.pallas_call(
        functools.partial(place_kernel, teams, head_dim),
        grid=(blocks,),
        in_specs=[VMEM] * (2 + teams),
        out_specs=[blocked(256, lambda s: s), blocked(width, lambda s: s)],
        out_shape=[
            jax.ShapeDtypeStruct((tokens, 256), BF16),
            jax.ShapeDtypeStruct((tokens, width), BF16),
        ],
        compiler_params=params(),
        cost_estimate=pl.CostEstimate(
            flops=2 * tokens * tokens * 384, bytes_accessed=tokens * 1600, transcendentals=0
        ),
        name="place",
    )(dest_bc, dt_bc, *pieces)

    down = lambda s: jnp.maximum(blocks - 1 - s, 0)
    after = lambda s: jnp.maximum(s - blocks, 0)
    up = lambda s: jnp.minimum(s, blocks - 1)
    du, grads, dx_sent = pl.pallas_call(
        functools.partial(back_kernel, blocks),
        grid=(2 * blocks,),
        in_specs=[
            SMEM, rowed(1, down), rowed(1, after), VMEM,
            blocked(256, down), blocked(width, down), blocked(width, down),
        ],
        out_specs=[
            blocked(width, down),
            pl.BlockSpec((1, 128, width), lambda s: (down(s), 0, 0)),
            blocked(width, after),
        ],
        out_shape=[
            jax.ShapeDtypeStruct((tokens, width), F32),
            jax.ShapeDtypeStruct((blocks, 128, width), F32),
            jax.ShapeDtypeStruct((tokens, width), BF16),
        ],
        scratch_shapes=[pltpu.VMEM((128, width), F32), pltpu.VMEM((tokens, width), BF16)],
        compiler_params=params(),
        cost_estimate=pl.CostEstimate(
            flops=2 * tokens * (tokens + 2000) * width,
            bytes_accessed=tokens * 3500,
            transcendentals=2 * tokens * width,
        ),
        name="back",
    )(docs, doc_row, dest_row, rate_row, bc_ctx, dt_ctx, dy_all)

    y_sent, dbc_part, ddt_part = pl.pallas_call(
        functools.partial(front_kernel, blocks, head_dim),
        grid=(2 * blocks,),
        in_specs=[
            SMEM, SMEM, rowed(1, up), VMEM, VMEM, VMEM, VMEM,
            blocked(256, up), blocked(width, up), blocked(width, up), blocked(width, up),
            pl.BlockSpec((1, 128, width), lambda s: (up(s), 0, 0)),
        ],
        out_specs=[blocked(width, up), blocked(256, after), rowed(padded, after)],
        out_shape=[
            jax.ShapeDtypeStruct((tokens, width), BF16),
            jax.ShapeDtypeStruct((tokens, 256), F32),
            jax.ShapeDtypeStruct((padded, tokens), F32),
        ],
        scratch_shapes=[
            pltpu.VMEM((128, width), F32),
            pltpu.VMEM((padded, 128), F32),
            pltpu.VMEM((tokens, 256), F32),
            pltpu.VMEM((tokens, 128), F32),
        ],
        compiler_params=params(),
        cost_estimate=pl.CostEstimate(
            flops=2 * tokens * (tokens + 4000) * width,
            bytes_accessed=tokens * 6000,
            transcendentals=2 * tokens * width,
        ),
        name="front",
    )(docs, destination, doc_row, dest_row, x_all, rate_row, rate_col, bc_ctx, dt_ctx, dy_all, du, grads)

    def from_channel(v):
        got = exchange(v).reshape(shards, rows_dev, width)
        return got.transpose(1, 0, 2).reshape(rows_dev, chan_dev)

    dx_load = from_channel(dx_sent)

    part = dbc_part.reshape(shards, teams, quarter, 256)
    reach = 1
    while reach < teams:
        size = part.shape[1]
        folded = part.reshape(shards, size // 2, 2, quarter, 256)
        bit = (team // reach) % 2
        keep = lax.dynamic_index_in_dim(folded, bit, 2, False)
        give = lax.dynamic_index_in_dim(folded, 1 - bit, 2, False)
        part = keep + lax.ppermute(give, "head", [(i, i ^ reach) for i in range(teams)])
        reach *= 2
    got = exchange(part.reshape(shards * quarter, 256)).reshape(shards, quarter, 256)
    mine = jnp.sum(got, axis=0).astype(BF16)
    shares = [mine] + [
        lax.ppermute(mine, "head", [(i, i ^ e) for i in range(teams)]) for e in range(1, teams)
    ]
    dbc_load = jnp.take(jnp.stack(shares), order, axis=0).reshape(rows_dev, 256)

    scan_output = from_channel(y_sent)
    ddt = ddt_part[:heads].reshape(heads, shards, rows_dev).transpose(1, 0, 2)
    ddt = exchange(ddt.reshape(shards * heads, rows_dev))
    ddt = jnp.sum(ddt.reshape(heads_dev, sharing, rows_dev), axis=1)
    return (scan_output, dx_load, dbc_load, ddt.T.astype(BF16))


def solution(mesh):
    return jax.shard_map(
        body,
        mesh=mesh,
        in_specs=(
            P("ctx", "head"),
            P("ctx", None),
            P("ctx", "head"),
            P("head"),
            P("ctx"),
            P(),
            P("ctx", "head"),
        ),
        out_specs=(P("ctx", "head"), P("ctx", "head"), P("ctx", None), P("ctx", "head")),
        check_vma=False,
    )
```

time: 796 us -> 399 us (0.50)
  local copies, waits for them, and re-layouts: 206 us -> 18.8 us
  Pallas kernels: 0 us -> 126 us
  waiting for transfers between devices: 267 us -> 168 us
  other arithmetic: 106 us -> 7.78 us
  matrix products: 89.5 us -> 0 us
  loops' own time: 20.7 us -> 0 us
  between operations: 17.1 us -> 0.95 us
  starting transfers between devices: 46 us -> 33.2 us
    all_to_all x6, waiting for transfers between devices: 267 us -> 125 us  [exchange(): return lax.all_to_all(v, 'ctx', split_axis=0, concat_axis=0, tiled=True)]
    pallas_call x0 -> x3, Pallas kernels: none -> 126 us  [the longest x1 68.3 us: body(): pl.pallas_call(functools.partial(front_kernel, blocks, head_dim), grid=(2...]
    dot_general x18 -> x0, matrix products: 82 us -> none  [the longest x2 23.9 us: intra_block(): y_local = jnp.einsum('hij,jhp->ihp', mixing, scaled, precision=PRECISE)]
    scatter x5 -> x0, local copies, waits for them, and re-layouts: 43.7 us -> none  [the longest x1 15.6 us: body(): jnp.zeros((total_slots,), jnp.int32).at[slot_back]]
    ppermute x0 -> x8, waiting for transfers between devices: none -> 42.9 us  [the longest x2 22.3 us: body(): lax.ppermute(give, 'head', [(i, i ^ reach) for i in range(teams)])]
    all_to_all x0 -> x2, blocking collectives: none -> 41.9 us  [exchange(): return lax.all_to_all(v, 'ctx', split_axis=0, concat_axis=0, tiled=True)]
    dynamic_slice x40 -> x2, local copies, waits for them, and re-layouts: 38.9 us -> 0.09 us  [the longest x1 0.08 us: body(): lax.dynamic_slice_in_dim(decay_rate, me * width // head_dim, heads)]
    add x13 -> x1, other arithmetic: 39.4 us -> 2.54 us  [body(): keep + lax.ppermute(give, 'head', [(i, i ^ reach) for i in range(teams)])]
  transfers between devices with their start and end apart: 8 -> 14, of which waited for: 4 -> 8; matrix products, arithmetic and copies ran while one was open for 37% -> 5% of each run, Pallas kernels for 0% -> 15%
where the time goes in v1:
time: 399 us; the launch traced here: 397 us
  waiting for transfers between devices  168 us (42%)
  Pallas kernels  126 us (32%)
  blocking collectives  41.9 us (11%)
  starting transfers between devices  33.2 us (8%)
  local copies, waits for them, and re-layouts  18.8 us (5%)
  other arithmetic  7.78 us (2%)
    all_to_all x6, waiting for transfers between devices, exchange(): return lax.all_to_all(v, 'ctx', split_axis=0, concat_axis=0, tiled=True)  125 us
    pallas_call x1, Pallas kernels, body(): pl.pallas_call(functools.partial(front_kernel, blocks, head_dim), grid=(2...  68.3 us
    all_to_all x2, blocking collectives, exchange(): return lax.all_to_all(v, 'ctx', split_axis=0, concat_axis=0, tiled=True)  41.9 us
    pallas_call x1, Pallas kernels, body(): pl.pallas_call(functools.partial(back_kernel, blocks), grid=(2 * blocks,)...  32.5 us
    all_to_all x6, starting transfers between devices, exchange(): return lax.all_to_all(v, 'ctx', split_axis=0, concat_axis=0, tiled=True)  27.3 us
    pallas_call x1, Pallas kernels, body(): pl.pallas_call(functools.partial(place_kernel, teams, head_dim), grid=(bl...  25.5 us
    ppermute x2, waiting for transfers between devices, body(): lax.ppermute(give, 'head', [(i, i ^ reach) for i in range(teams)])  22.3 us
    ppermute x3, waiting for transfers between devices, body(): lax.ppermute(part_bc, 'head', [(i, i ^ e) for i in range(teams)])  20.7 us
  transfers between devices with their start and end apart: 14, of which 8 were waited for; matrix products, arithmetic and copies ran while one was open for 5% of the time, Pallas kernels for 15%

profile of v1, /device:TPU:0, one launch (start us, length us, event | category | flops | bytes accessed | tf_op | source)
XLA Modules:
  0.0 397.4 jit_solution(17421506421683480672)
XLA Ops:
  0.7 1.5 gather_fusion
  2.2 0.7 convert_element_type.44
  3.0 0.7 pad_maximum_fusion.1
  3.6 7.3 %all-to-all-start = ((bf16[8,5,512]{2,1,0:T(8,128)(2,1)}), bf16[8,5,512]{2,1,0:T(8,128)(2,1)S(1)}, u32[]{:S(2)}, u32[]{:S(2)}) async-start(bf16[8,5,512]{2,1,0:T(8,128)(2,1)} %pad_maximum_fusion.1), calls=%async_computation | async-start | bytes 131072 | tf_op jit(solution)/shard_map/all_to_all | solution.py:235
  10.9 6.9 %all-to-all-done = bf16[8,5,512]{2,1,0:T(8,128)(2,1)S(1)} async-done(((bf16[8,5,512]{2,1,0:T(8,128)(2,1)}), bf16[8,5,512]{2,1,0:T(8,128)(2,1)S(1)}, u32[]{:S(2)}, u32[]{:S(2)}) %all-to-all-start) | async-done | bytes 40992 | tf_op jit(solution)/shard_map/all_to_all | solution.py:235
  17.8 0.8 broadcast_in_dim.68
  18.6 3.5 all-to-all-start.2
  22.1 1.5 copy.64
  23.6 11.8 %all-to-all-done.2 = bf16[8,128,256]{2,1,0:T(8,128)(2,1)S(1)} async-done(((bf16[8,128,256]{2,1,0:T(8,128)(2,1)}), bf16[8,128,256]{2,1,0:T(8,128)(2,1)S(1)}, u32[]{:S(2)}, u32[]{:S(2)}) %all-to-all-start.2) | async-done | bytes 524320 | tf_op jit(solution)/shard_map/all_to_all | solution.py:235
  35.4 4.6 %all-to-all-start.3 = ((bf16[8,512,256]{2,1,0:T(8,128)(2,1)}), bf16[8,512,256]{2,1,0:T(8,128)(2,1)}, u32[]{:S(2)}, u32[]{:S(2)}) async-start(bf16[8,512,256]{2,1,0:T(8,128)(2,1)} %bitcast.71), calls=%async_computation.3 | async-start | bytes 4194304 | tf_op jit(solution)/shard_map/all_to_all | solution.py:235
  40.0 1.5 copy.65
  41.5 45.5 %all-to-all-done.3 = bf16[8,512,256]{2,1,0:T(8,128)(2,1)} async-done(((bf16[8,512,256]{2,1,0:T(8,128)(2,1)}), bf16[8,512,256]{2,1,0:T(8,128)(2,1)}, u32[]{:S(2)}, u32[]{:S(2)}) %all-to-all-start.3) | async-done | bytes 2097184 | tf_op jit(solution)/shard_map/all_to_all | solution.py:235
  87.0 3.8 all-to-all-start.1
  90.9 0.7 broadcast_in_dim_reshape.4.rate_ref
  91.7 0.6 gather_fusion.1
  92.3 0.7 broadcast_select_fusion
  93.0 1.5 collective-permute-start.1
  94.5 0.3 collective-permute-start.2
  94.9 0.7 copy.49.rate_col
  95.6 0.6 gather_fusion.2
  96.2 0.7 concatenate.32.dt_ref
  96.9 0.6 slice_convert_fusion
  97.5 10.4 %collective-permute-done.1.refs_2_ = bf16[1024,256]{1,0:T(8,128)(2,1)} collective-permute-done((bf16[1024,256]{1,0:T(8,128)(2,1)S(1)}, bf16[1024,256]{1,0:T(8,128)(2,1)}, u32[]{:S(2)}, u32[]{:S(2)}) %collective-permute-start.1) | collective-permute-done | bytes 524320 | tf_op jit(solution)/shard_map/ppermute | solution.py:253
  107.9 10.3 %collective-permute-done.2.refs_3_ = bf16[1024,256]{1,0:T(8,128)(2,1)} collective-permute-done((bf16[1024,256]{1,0:T(8,128)(2,1)S(1)}, bf16[1024,256]{1,0:T(8,128)(2,1)}, u32[]{:S(2)}, u32[]{:S(2)}) %collective-permute-start.2) | collective-permute-done | bytes 524320 | tf_op jit(solution)/shard_map/ppermute | solution.py:253
  118.2 25.5 %place.1 = (bf16[4096,256]{1,0:T(8,128)(2,1)}, bf16[4096,256]{1,0:T(8,128)(2,1)}) custom-call(s32[1,4096]{1,0:T(1,128)} %bitcast.101, bf16[16,4096]{1,0:T(8,128)(2,1)} %concatenate.32.dt_ref, bf16[1024,256]{1,0:T(8,128)(2,1)} %bitcast.89, bf16[1024,256]{1,0:T(8,128)(2,1)} %collective-permute-done.refs_1_, bf16[1024,256]{1,0:T(8,128)(2,1)} %collective-permute-done.1.refs_2_, ...), custom_call_target="tpu_custom_call" | custom-call | flops 12884901888 | bytes 6553600 | tf_op jit(solution)/shard_map/place/pallas_call | solution.py:275
  143.7 32.5 %back.1 = (f32[4096,256]{1,0:T(8,128)}, f32[16,128,256]{2,1,0:T(8,128)}, bf16[4096,256]{1,0:T(8,128)(2,1)}) custom-call(f32[4096]{0:T(1024)} %bitcast.102, f32[1,4096]{1,0:T(1,128)} %bitcast.103, s32[1,4096]{1,0:T(1,128)} %bitcast.98, f32[1,256]{1,0:T(1,128)} %broadcast_in_dim_reshape.4.rate_ref, bf16[4096,256]{1,0:T(8,128)(2,1)} %get-tuple-element.12.bc_ref, ...), custom_call_target="tpu_custom_call" | custom-call | flops 12784238592 | bytes 14336000 | tf_op jit(solution)/shard_map/back/pallas_call | solution.py:294
  176.3 1.3 copy-done.4
  177.6 68.3 %front.1 = (bf16[4096,256]{1,0:T(8,128)(2,1)}, f32[4096,256]{1,0:T(8,128)}, f32[8,4096]{1,0:T(8,128)}) custom-call(f32[4096]{0:T(1024)} %bitcast.104, s32[4096]{0:T(1024)} %dest_smem.1, f32[1,4096]{1,0:T(1,128)} %bitcast.105, s32[1,4096]{1,0:T(1,128)} %bitcast.99, bf16[4096,256]{1,0:T(8,128)(2,1)} %bitcast.82, f32[1,256]{1,0:T(1,128)} %broadcast_in_dim_reshape.4.rate_ref, ...), custom_call_target="tpu_custom_call" | custom-call | flops 16978542592 | bytes 24576000 | tf_op jit(solution)/shard_map/front/pallas_call | solution.py:321
  245.9 1.8 dynamic-slice_bitcast_fusion
  247.7 0.5 collective-permute-start.3
  248.2 0.9 slice.11
  249.1 12.5 %all_to_all.63 = bf16[8,4,512]{2,1,0:T(4,128)(2,1)S(1)} all-to-all(bf16[8,4,512]{2,1,0:T(4,128)(2,1)S(1)} %bitcast.93), channel_id=1, replica_groups=mesh['ctx'=8,'head'=4] {'ctx'}, dimensions={0} | all-to-all | bytes 65536 | tf_op jit(solution)/shard_map/all_to_all | solution.py:235
  261.6 4.4 %all-to-all-start.4 = ((bf16[8,512,256]{2,1,0:T(8,128)(2,1)}), bf16[8,512,256]{2,1,0:T(8,128)(2,1)}, u32[]{:S(2)}, u32[]{:S(2)}) async-start(bf16[8,512,256]{2,1,0:T(8,128)(2,1)} %bitcast.24), calls=%async_computation.4 | async-start | bytes 4194304 | tf_op jit(solution)/shard_map/all_to_all | solution.py:235
  266.0 2.5 bitcast_add_fusion
  268.7 1.6 collective-permute-start.4
  270.3 22.3 %collective-permute-done.4 = f32[8,1,128,256]{3,2,1,0:T(8,128)} collective-permute-done((f32[8,1,128,256]{3,2,1,0:T(8,128)S(1)}, f32[8,1,128,256]{3,2,1,0:T(8,128)}, u32[]{:S(2)}, u32[]{:S(2)}) %collective-permute-start.4) | collective-permute-done | bytes 1048608 | tf_op jit(solution)/shard_map/ppermute | solution.py:364
  292.5 1.4 add_bitcast_fusion
  293.9 19.3 %all-to-all-done.4 = bf16[8,512,256]{2,1,0:T(8,128)(2,1)} async-done(((bf16[8,512,256]{2,1,0:T(8,128)(2,1)}), bf16[8,512,256]{2,1,0:T(8,128)(2,1)}, u32[]{:S(2)}, u32[]{:S(2)}) %all-to-all-start.4) | async-done | bytes 2097184 | tf_op jit(solution)/shard_map/all_to_all | solution.py:235
  313.2 29.4 %all_to_all.64 = f32[8,128,256]{2,1,0:T(8,128)} all-to-all(f32[8,128,256]{2,1,0:T(8,128)S(1)} %add_bitcast_fusion), channel_id=1, replica_groups=mesh['ctx'=8,'head'=4] {'ctx'}, dimensions={0} | all-to-all | bytes 2097152 | tf_op jit(solution)/shard_map/all_to_all | solution.py:235
  342.6 3.8 all-to-all-start.5
  346.6 1.6 collective-permute-start.6
  348.2 0.3 collective-permute-start.7
  348.5 0.6 convert_element_type.52
  349.1 3.2 copy.56
  352.3 42.0 %all-to-all-done.5 = bf16[8,512,256]{2,1,0:T(8,128)(2,1)S(1)} async-done(((bf16[8,512,256]{2,1,0:T(8,128)(2,1)}), bf16[8,512,256]{2,1,0:T(8,128)(2,1)S(1)}, u32[]{:S(2)}, u32[]{:S(2)}) %all-to-all-start.5) | async-done | bytes 2097184 | tf_op jit(solution)/shard_map/all_to_all | solution.py:235
  394.3 1.6 copy.57
  396.0 0.6 gather_fusion.3
  396.5 0.8 bitcast_select_fusion
  (43 shorter events, 0.9 us)
Async XLA Ops:
  0.6 10.3 %copy-start = (bf16[512,256]{1,0:T(8,128)(2,1)S(1)}, bf16[512,256]{1,0:T(8,128)(2,1)}, u32[]{:S(2)}) copy-start(bf16[512,256]{1,0:T(8,128)(2,1)} %param.9) | copy-start | bytes 786436
  0.6 21.5 %copy-start.2 = (bf16[512,2048]{1,0:T(8,128)(2,1)S(1)}, bf16[512,2048]{1,0:T(8,128)(2,1)}, u32[]{:S(2)}) copy-start(bf16[512,2048]{1,0:T(8,128)(2,1)} %param.14) | copy-start | bytes 6291460
  3.6 14.2 %all-to-all-start = ((bf16[8,5,512]{2,1,0:T(8,128)(2,1)}), bf16[8,5,512]{2,1,0:T(8,128)(2,1)S(1)}, u32[]{:S(2)}, u32[]{:S(2)}) async-start(bf16[8,5,512]{2,1,0:T(8,128)(2,1)} %pad_maximum_fusion.1), calls=%async_computation | async-start | bytes 131072 | tf_op jit(solution)/shard_map/all_to_all | solution.py:235
  18.6 16.8 %all-to-all-start.2 = ((bf16[8,128,256]{2,1,0:T(8,128)(2,1)}), bf16[8,128,256]{2,1,0:T(8,128)(2,1)S(1)}, u32[]{:S(2)}, u32[]{:S(2)}) async-start(bf16[8,128,256]{2,1,0:T(8,128)(2,1)} %broadcast_in_dim.68), calls=%async_computation.2 | async-start | bytes 1048576 | tf_op jit(solution)/shard_map/all_to_all | solution.py:235
  35.4 59.1 %copy-start.5 = (bf16[8,128,256]{2,1,0:T(8,128)(2,1)}, bf16[8,128,256]{2,1,0:T(8,128)(2,1)S(1)}, u32[]{:S(2)}) copy-start(bf16[8,128,256]{2,1,0:T(8,128)(2,1)S(1)} %all-to-all-done.2) | copy-start | bytes 1572868
  35.4 4.6 %copy-start.3 = (bf16[512,2048]{1,0:T(8,128)(2,1)S(1)}, bf16[512,2048]{1,0:T(8,128)(2,1)}, u32[]{:S(2)}) copy-start(bf16[512,2048]{1,0:T(8,128)(2,1)} %param.8) | copy-start | bytes 6291460
  35.4 51.6 %all-to-all-start.3 = ((bf16[8,512,256]{2,1,0:T(8,128)(2,1)}), bf16[8,512,256]{2,1,0:T(8,128)(2,1)}, u32[]{:S(2)}, u32[]{:S(2)}) async-start(bf16[8,512,256]{2,1,0:T(8,128)(2,1)} %bitcast.71), calls=%async_computation.3 | async-start | bytes 4194304 | tf_op jit(solution)/shard_map/all_to_all | solution.py:235
  87.0 3.8 copy-start.6
  87.0 3.8 copy-start.7
  87.0 89.3 %all-to-all-start.1 = ((bf16[8,512,256]{2,1,0:T(8,128)(2,1)}), bf16[8,512,256]{2,1,0:T(8,128)(2,1)S(1)}, u32[]{:S(2)}, u32[]{:S(2)}) async-start(bf16[8,512,256]{2,1,0:T(8,128)(2,1)} %bitcast.73), calls=%async_computation.1 | async-start | bytes 4194304 | tf_op jit(solution)/shard_map/all_to_all | solution.py:235
  93.0 4.5 %collective-permute-start = (bf16[1024,256]{1,0:T(8,128)(2,1)S(1)}, bf16[1024,256]{1,0:T(8,128)(2,1)}, u32[]{:S(2)}, u32[]{:S(2)}) collective-permute-start(bf16[1024,256]{1,0:T(8,128)(2,1)S(1)} %bitcast.86), channel_id=1, source_target_pairs={{0,1},{1,0},{2,3},{3,2},{4,5},{5,4},{6,7},{7,6},{8,9},{9,8},{10,11... | collective-permute-start | bytes 1572872 | tf_op jit(solution)/shard_map/ppermute | solution.py:253
  93.0 14.9 %collective-permute-start.1 = (bf16[1024,256]{1,0:T(8,128)(2,1)S(1)}, bf16[1024,256]{1,0:T(8,128)(2,1)}, u32[]{:S(2)}, u32[]{:S(2)}) collective-permute-start(bf16[1024,256]{1,0:T(8,128)(2,1)S(1)} %bitcast.87), channel_id=1, source_target_pairs={{0,2},{1,3},{2,0},{3,1},{4,6},{5,7},{6,4},{7,5},{8,10},{9,11},{10,... | collective-permute-start | bytes 1572872 | tf_op jit(solution)/shard_map/ppermute | solution.py:253
  94.5 23.7 %collective-permute-start.2 = (bf16[1024,256]{1,0:T(8,128)(2,1)S(1)}, bf16[1024,256]{1,0:T(8,128)(2,1)}, u32[]{:S(2)}, u32[]{:S(2)}) collective-permute-start(bf16[1024,256]{1,0:T(8,128)(2,1)S(1)} %bitcast.88), channel_id=1, source_target_pairs={{0,3},{1,2},{2,1},{3,0},{4,7},{5,6},{6,5},{7,4},{8,11},{9,10},{10,... | collective-permute-start | bytes 1572872 | tf_op jit(solution)/shard_map/ppermute | solution.py:253
  176.3 1.3 copy-start.4
  247.7 18.3 %collective-permute-start.3 = (f32[8,2,128,256]{3,2,1,0:T(8,128)S(1)}, f32[8,2,128,256]{3,2,1,0:T(8,128)}, u32[]{:S(2)}, u32[]{:S(2)}) collective-permute-start(f32[8,2,128,256]{3,2,1,0:T(8,128)S(1)} %dynamic-slice_bitcast_fusion), channel_id=1, source_target_pairs={{0,1},{1,0},{2,3},{3,2},{4,5},{5,4},{6,7},{7,6},{8,9},{9,8},{10,11... | collective-permute-start | bytes 6291464 | tf_op jit(solution)/shard_map/ppermute | solution.py:364
  261.6 51.6 %all-to-all-start.4 = ((bf16[8,512,256]{2,1,0:T(8,128)(2,1)}), bf16[8,512,256]{2,1,0:T(8,128)(2,1)}, u32[]{:S(2)}, u32[]{:S(2)}) async-start(bf16[8,512,256]{2,1,0:T(8,128)(2,1)} %bitcast.24), calls=%async_computation.4 | async-start | bytes 4194304 | tf_op jit(solution)/shard_map/all_to_all | solution.py:235
  268.7 23.8 %collective-permute-start.4 = (f32[8,1,128,256]{3,2,1,0:T(8,128)S(1)}, f32[8,1,128,256]{3,2,1,0:T(8,128)}, u32[]{:S(2)}, u32[]{:S(2)}) collective-permute-start(f32[8,1,128,256]{3,2,1,0:T(8,128)S(1)} %constant_dynamic-slice_fusion.1), channel_id=1, source_target_pairs={{0,2},{1,3},{2,0},{3,1},{4,6},{5,7},{6,4},{7,5},{8,10},{9,11},{10,... | collective-permute-start | bytes 3145736 | tf_op jit(solution)/shard_map/ppermute | solution.py:364
  342.6 3.8 copy-start.1
  342.6 51.7 %all-to-all-start.5 = ((bf16[8,512,256]{2,1,0:T(8,128)(2,1)}), bf16[8,512,256]{2,1,0:T(8,128)(2,1)S(1)}, u32[]{:S(2)}, u32[]{:S(2)}) async-start(bf16[8,512,256]{2,1,0:T(8,128)(2,1)} %bitcast.83), calls=%async_computation.5 | async-start | bytes 4194304 | tf_op jit(solution)/shard_map/all_to_all | solution.py:235
  346.5 49.4 %collective-permute-start.5 = (bf16[128,256]{1,0:T(8,128)(2,1)S(1)}, bf16[128,256]{1,0:T(8,128)(2,1)S(1)}, u32[]{:S(2)}, u32[]{:S(2)}) collective-permute-start(bf16[128,256]{1,0:T(8,128)(2,1)S(1)} %reduce_sum.8), channel_id=1, source_target_pairs={{0,1},{1,0},{2,3},{3,2},{4,5},{5,4},{6,7},{7,6},{8,9},{9,8},{10,11... | collective-permute-start | bytes 196616 | tf_op jit(solution)/shard_map/ppermute | solution.py:369
  346.6 49.3 %collective-permute-start.6 = (bf16[128,256]{1,0:T(8,128)(2,1)S(1)}, bf16[128,256]{1,0:T(8,128)(2,1)S(1)}, u32[]{:S(2)}, u32[]{:S(2)}) collective-permute-start(bf16[128,256]{1,0:T(8,128)(2,1)S(1)} %reduce_sum.8), channel_id=1, source_target_pairs={{0,2},{1,3},{2,0},{3,1},{4,6},{5,7},{6,4},{7,5},{8,10},{9,11},{10,... | collective-permute-start | bytes 196616 | tf_op jit(solution)/shard_map/ppermute | solution.py:369
  348.2 47.8 %collective-permute-start.7 = (bf16[128,256]{1,0:T(8,128)(2,1)S(1)}, bf16[128,256]{1,0:T(8,128)(2,1)S(1)}, u32[]{:S(2)}, u32[]{:S(2)}) collective-permute-start(bf16[128,256]{1,0:T(8,128)(2,1)S(1)} %reduce_sum.8), channel_id=1, source_target_pairs={{0,3},{1,2},{2,1},{3,0},{4,7},{5,6},{6,5},{7,4},{8,11},{9,10},{10,... | collective-permute-start | bytes 196616 | tf_op jit(solution)/shard_map/ppermute | solution.py:369

commit v2 on v1

v2 whole, which is shorter than its diff:
```python
import functools
import jax
import jax.numpy as jnp
from jax import lax
from jax.experimental import pallas as pl
from jax.experimental.pallas import tpu as pltpu
from jax.sharding import PartitionSpec as P


BLOCK = 256
PLACE = 1024
F32, BF16, I32 = jnp.float32, jnp.bfloat16, jnp.int32
NN, NT, TN = (((1,), (0,)), ((), ())), (((1,), (1,)), ((), ())), (((0,), (0,)), ((), ()))
VMEM = pl.BlockSpec(memory_space=pltpu.VMEM)
SMEM = pl.BlockSpec(memory_space=pltpu.SMEM)


def dot(a, b, dims=NN):
    return lax.dot_general(a, b, dims, preferred_element_type=F32)


def split2(v):
    hi = v.astype(BF16)
    return hi, (v - hi.astype(F32)).astype(BF16)


def expander(heads, width, head_dim):
    h = lax.broadcasted_iota(I32, (heads, width), 0)
    c = lax.broadcasted_iota(I32, (heads, width), 1)
    return jnp.where(c // head_dim == h, 1.0, 0.0).astype(BF16)


def place_kernel(pieces, head_dim, dest_ref, dt_ref, *refs):
    bc_refs, (bc_out, dt_out) = refs[:pieces], refs[pieces:]
    size = bc_refs[0].shape[0]
    block = bc_out.shape[0]
    first = pl.program_id(0) * block
    acc_bc = jnp.zeros((block, bc_out.shape[1]), F32)
    acc_dt = jnp.zeros((block, dt_ref.shape[0]), F32)
    for e in range(pieces):
        here = lax.broadcasted_iota(I32, (block, size), 0) + first
        pick = jnp.where(here == dest_ref[:, e * size : (e + 1) * size], 1.0, 0.0).astype(BF16)
        acc_bc = acc_bc + dot(pick, bc_refs[e][...])
        acc_dt = acc_dt + dot(pick, dt_ref[:, e * size : (e + 1) * size], NT)
    bc_out[...] = acc_bc.astype(BF16)
    spread = expander(dt_ref.shape[0], dt_out.shape[1], head_dim)
    dt_out[...] = dot(acc_dt.astype(BF16), spread).astype(BF16)


def constants(lower_ref, spread_ref, head_dim):
    rows = lax.broadcasted_iota(I32, (BLOCK, BLOCK), 0)
    cols = lax.broadcasted_iota(I32, (BLOCK, BLOCK), 1)
    lower_ref[...] = jnp.where(rows >= cols, 1.0, 0.0).astype(BF16)
    if spread_ref is not None:
        width = spread_ref.shape[0] // 2
        c = lax.broadcasted_iota(I32, (width, 128), 0)
        h = lax.broadcasted_iota(I32, (width, 128), 1)
        one = jnp.where(c // head_dim == h, 1.0, 0.0).astype(BF16)
        spread_ref[...] = jnp.concatenate([one] * 2, axis=0)


def decays(dt_ref, rate_ref, lower_ref):
    running = rate_ref[...] * dot(lower_ref[...], dt_ref[...])
    return jnp.exp(-running), jnp.exp(running), jnp.exp(-running[BLOCK - 1 :, :])


def doc_state(doc_smem, block):
    last = doc_smem[block * BLOCK + BLOCK - 1]
    prev = jnp.where(block == 0, -1.0, doc_smem[jnp.maximum(block * BLOCK - 1, 0)])
    return prev, last


def only(cond, v):
    return jnp.where(cond, v.astype(F32), 0.0).astype(BF16)


def lanes(*parts):
    return jnp.concatenate(parts, axis=1)


def stack(*parts):
    return jnp.concatenate(parts, axis=0)


def fore_kernel(
    doc_smem, doc_ref, doc_col, dest_ref, x_ref, rate_ref, bc_ref, dt_ref,
    y_out, yf_out, x_out, state_out, state_ref, lower_ref,
):
    block = pl.program_id(0)

    @pl.when(block == 0)
    def _():
        state_ref[...] = jnp.zeros_like(state_ref)
        constants(lower_ref, None, None)

    tokens = x_ref.shape[0]
    here = lax.broadcasted_iota(I32, (BLOCK, tokens), 0) + block * BLOCK
    pick = jnp.where(here == dest_ref[...], 1.0, 0.0).astype(BF16)
    x = dot(pick, x_ref[...])
    x_out[...] = x.astype(BF16)
    b, c = bc_ref[:, :128], bc_ref[:, 128:]
    enter, leave, total = decays(dt_ref, rate_ref, lower_ref)
    prev, last = doc_state(doc_smem, block)
    row, col = doc_ref[...], doc_col[...]
    rows = lax.broadcasted_iota(I32, (BLOCK, BLOCK), 0)
    cols = lax.broadcasted_iota(I32, (BLOCK, BLOCK), 1)
    earlier = (col == row) & (rows >= cols)
    ah, al = split2(jnp.where(earlier, dot(c, b, NT), 0.0))
    uh, ul = split2(leave * (dt_ref[...].astype(F32) * x))
    state = state_ref[...]
    state_out[0] = state
    sh, sl = split2(state)
    c_first = only(col == prev, c)
    y = enter * dot(lanes(ah, ah, al, c_first, c_first), stack(uh, ul, uh, sh, sl))
    yf_out[...] = y
    y_out[...] = y.astype(BF16)
    b_last = only(col == last, b)
    fresh = dot(stack(b_last, b_last), stack(uh, ul), TN)
    state_ref[...] = total * (jnp.where(prev == last, state, 0.0) + fresh)


def back_kernel(
    blocks, head_dim, doc_smem, side_smem, doc_ref, doc_col, rate_ref, rate_lane,
    bc_ref, dt_ref, x_ref, dy_ref, y_ref, state_ref,
    dx_out, keep_out, give_out, ddt_out,
    grad_ref, sum_ref, lower_ref, spread_ref,
):
    step = pl.program_id(0)

    @pl.when(step == 0)
    def _():
        grad_ref[...] = jnp.zeros_like(grad_ref)
        sum_ref[...] = jnp.zeros_like(sum_ref)
        constants(lower_ref, spread_ref, head_dim)

    block = blocks - 1 - step
    b, c = bc_ref[:, :128], bc_ref[:, 128:]
    enter, leave, total = decays(dt_ref, rate_ref, lower_ref)
    prev, last = doc_state(doc_smem, block)
    row, col = doc_ref[...], doc_col[...]
    rows = lax.broadcasted_iota(I32, (BLOCK, BLOCK), 0)
    cols = lax.broadcasted_iota(I32, (BLOCK, BLOCK), 1)
    later = (col == row) & (cols >= rows)
    is_last, is_first = col == last, col == prev
    ah, al = split2(jnp.where(later, dot(b, c, NT), 0.0))
    dt = dt_ref[...].astype(F32)
    x = x_ref[...].astype(F32)
    dy = dy_ref[...].astype(F32)
    gh, gl = split2(enter * dy)
    uh, ul = split2(leave * (dt * x))
    grad = total * grad_ref[...]
    rh, rl = split2(grad)
    sh, sl = split2(state_ref[0])
    b_last, c_first = only(is_last, b), only(is_first, c)
    du = leave * dot(lanes(ah, ah, al, b_last, b_last), stack(gh, gl, gh, rh, rl))
    dx = dt * du
    dx_out[...] = dx.astype(BF16)
    fresh = dot(stack(c_first, c_first), stack(gh, gl), TN)
    grad_ref[...] = jnp.where(prev == last, grad, 0.0) + fresh
    g3, u3 = lanes(gh, gl, gh), lanes(uh, uh, ul)
    qh, qlow = split2(jnp.where(later, dot(u3, g3, NT), 0.0))
    dc = dot(stack(qh, qlow), stack(b, b), TN)
    dc = dc + jnp.where(is_first, dot(g3, lanes(sh, sh, sl), NT), 0.0)
    db = dot(lanes(qh, qlow), stack(c, c))
    db = db + jnp.where(is_last, dot(u3, lanes(rh, rl, rh), NT), 0.0)
    side = side_smem[0] == 0
    keep_out[...] = jnp.where(side, db, dc)
    give_out[...] = jnp.where(side, dc, db)
    spread = spread_ref[...]
    balance = dot(lanes(*split2(dy * y_ref[...] - x * dx)), spread)
    mask = jnp.where(later, 1.0, 0.0).astype(BF16)
    suffix = dot(lanes(mask, mask), stack(*split2(balance)))
    suffix = suffix + jnp.where(is_last, sum_ref[:1, :], 0.0)
    sum_ref[...] = jnp.broadcast_to(
        jnp.where(prev == doc_smem[block * BLOCK], suffix[:1, :], 0.0), sum_ref.shape
    )
    ddt_out[...] = dot(lanes(*split2(x * du)), spread) - rate_lane[...] * suffix


def pick8(dest_smem, source, target, base):
    def rows8(i, carry):
        at = pl.multiple_of(i * 8, 8)
        spots = [dest_smem[base + at + j] for j in range(8)]
        target[pl.ds(at, 8), :] = stack(*[source[pl.ds(s, 1), :] for s in spots])
        return carry

    lax.fori_loop(0, target.shape[0] // 8, rows8, 0, unroll=4)


def rows_kernel(dest_smem, keep_ref, more_ref, dbc_out, sum_ref):
    sum_ref[...] = keep_ref[...] + more_ref[...]
    pick8(dest_smem, sum_ref, dbc_out, 0)


def turn_kernel(dest_smem, ddt_ref, ddt_out, small_ref):
    pick8(dest_smem, ddt_ref, small_ref, pl.program_id(0) * BLOCK)
    ddt_out[...] = small_ref[...].T[: ddt_out.shape[0], :]


def gather_kernel(dest_col, dx_ref, dx_out):
    here = lax.broadcasted_iota(I32, (dx_out.shape[0], dx_ref.shape[0]), 1)
    pick = jnp.where(here == dest_col[...], 1.0, 0.0).astype(BF16)
    dx_out[...] = dot(pick, dx_ref[...]).astype(BF16)


def params(**extra):
    return pltpu.CompilerParams(
        dimension_semantics=("arbitrary",), vmem_limit_bytes=60 << 20, **extra
    )


def struct(dtype, *shape):
    return jax.ShapeDtypeStruct(shape, dtype)


def blocked(cols, index, size=BLOCK):
    return pl.BlockSpec((size, cols), lambda s: (index(s), 0))


def rowed(rows, index):
    return pl.BlockSpec((rows, BLOCK), lambda s: (0, index(s)))


def planes(width, index):
    return pl.BlockSpec((1, 128, width), lambda s: (index(s), 0, 0))


def place(dest_bc, dt_bc, pieces, width, head_dim):
    tokens = dest_bc.shape[1]
    same = lambda s: s
    return pl.pallas_call(
        functools.partial(place_kernel, len(pieces), head_dim),
        grid=(tokens // PLACE,),
        in_specs=[VMEM] * (2 + len(pieces)),
        out_specs=[blocked(256, same, PLACE), blocked(width, same, PLACE)],
        out_shape=[struct(BF16, tokens, 256), struct(BF16, tokens, width)],
        compiler_params=params(),
        cost_estimate=pl.CostEstimate(
            flops=2 * tokens * tokens * 384, bytes_accessed=tokens * 1600, transcendentals=0
        ),
        name="place",
    )(dest_bc, dt_bc, *pieces)


def fore(docs, destination, x_all, rate_row, bc_ctx, dt_ctx):
    tokens, width = x_all.shape
    blocks = tokens // BLOCK
    same = lambda s: s
    return pl.pallas_call(
        fore_kernel,
        grid=(blocks,),
        in_specs=[
            SMEM, rowed(1, same), blocked(1, same), VMEM, VMEM, VMEM,
            blocked(256, same), blocked(width, same),
        ],
        out_specs=[blocked(width, same)] * 3 + [planes(width, same)],
        out_shape=[
            struct(BF16, tokens, width),
            struct(F32, tokens, width),
            struct(BF16, tokens, width),
            struct(F32, blocks, 128, width),
        ],
        scratch_shapes=[pltpu.VMEM((128, width), F32), pltpu.VMEM((BLOCK, BLOCK), BF16)],
        compiler_params=params(),
        cost_estimate=pl.CostEstimate(
            flops=2 * tokens * (tokens + 2000) * width,
            bytes_accessed=tokens * 4000,
            transcendentals=2 * tokens * width,
        ),
        name="fore",
    )(docs, docs[None], docs[:, None], destination[None], x_all, rate_row, bc_ctx, dt_ctx)


def back(docs, side, rate_row, rate_lane, bc_ctx, dt_ctx, x_ctx, dy_all, y_all, states, head_dim):
    tokens, width = x_ctx.shape
    blocks = tokens // BLOCK
    down = lambda s: blocks - 1 - s
    return pl.pallas_call(
        functools.partial(back_kernel, blocks, head_dim),
        grid=(blocks,),
        in_specs=[
            SMEM, SMEM, rowed(1, down), blocked(1, down), VMEM, VMEM,
            blocked(256, down), blocked(width, down), blocked(width, down),
            blocked(width, down), blocked(width, down), planes(width, down),
        ],
        out_specs=[blocked(width, down)] + [blocked(128, down)] * 3,
        out_shape=[struct(BF16, tokens, width)] + [struct(F32, tokens, 128)] * 3,
        scratch_shapes=[
            pltpu.VMEM((128, width), F32),
            pltpu.VMEM((8, 128), F32),
            pltpu.VMEM((BLOCK, BLOCK), BF16),
            pltpu.VMEM((2 * width, 128), BF16),
        ],
        compiler_params=params(),
        cost_estimate=pl.CostEstimate(
            flops=2 * tokens * 4000 * width,
            bytes_accessed=tokens * 6000,
            transcendentals=2 * tokens * width,
        ),
        name="back",
    )(
        docs, side, docs[None], docs[:, None], rate_row, rate_lane,
        bc_ctx, dt_ctx, x_ctx, dy_all, y_all, states,
    )


def gather_rows(spots, keep, more):
    return pl.pallas_call(
        rows_kernel,
        in_specs=[SMEM, VMEM, VMEM],
        out_specs=VMEM,
        out_shape=struct(F32, spots.shape[0], 128),
        scratch_shapes=[pltpu.VMEM(keep.shape, F32)],
        compiler_params=pltpu.CompilerParams(vmem_limit_bytes=60 << 20),
        cost_estimate=pl.CostEstimate(
            flops=keep.size, bytes_accessed=keep.size * 12, transcendentals=0
        ),
        name="gather_rows",
    )(spots, keep, more)


def gather_turn(destination, ddt, heads):
    tokens = ddt.shape[0]
    padded = -(-heads // 8) * 8
    return pl.pallas_call(
        turn_kernel,
        grid=(tokens // BLOCK,),
        in_specs=[SMEM, VMEM],
        out_specs=rowed(padded, lambda s: s),
        out_shape=struct(F32, padded, tokens),
        scratch_shapes=[pltpu.VMEM((BLOCK, 128), F32)],
        compiler_params=params(),
        cost_estimate=pl.CostEstimate(
            flops=tokens * 256, bytes_accessed=tokens * 1000, transcendentals=0
        ),
        name="gather_turn",
    )(destination, ddt)


def gather_back(destination, dx_ctx, shards):
    tokens, width = dx_ctx.shape
    size = tokens // shards
    return pl.pallas_call(
        gather_kernel,
        grid=(shards,),
        in_specs=[blocked(1, lambda s: s, size), VMEM],
        out_specs=blocked(width, lambda s: s, size),
        out_shape=struct(BF16, tokens, width),
        compiler_params=params(),
        cost_estimate=pl.CostEstimate(
            flops=2 * tokens * tokens * width, bytes_accessed=tokens * 1500, transcendentals=0
        ),
        name="gather_back",
    )(destination[:, None], dx_ctx)


def after(value, *others):
    return lax.optimization_barrier((value,) + others)[0]


def body(x_load, bc_load, dt_load, decay_rate, doc_ids, destination, grad_y):
    shards, teams = lax.axis_size("ctx"), lax.axis_size("head")
    me, team = lax.axis_index("ctx"), lax.axis_index("head")
    rows_dev, chan_dev = x_load.shape
    heads_dev = dt_load.shape[1]
    head_dim = chan_dev // heads_dev
    width = chan_dev // shards
    tokens = rows_dev * shards
    heads = max(1, width // head_dim)
    sharing = shards * heads // heads_dev
    quarter = rows_dev // teams

    def exchange(v):
        return lax.all_to_all(v, "ctx", split_axis=0, concat_axis=0, tiled=True)

    def ring(v, reach):
        return lax.ppermute(v, "ctx", [(i, i ^ reach) for i in range(shards)])

    def across(v, reach):
        return lax.ppermute(v, "head", [(i, i ^ reach) for i in range(teams)])

    def by_channel(v):
        parts = v.reshape(rows_dev, shards, width).transpose(1, 0, 2)
        return parts.reshape(tokens, width)

    def from_channel(got):
        got = got.reshape(shards, rows_dev, width)
        return got.transpose(1, 0, 2).reshape(rows_dev, chan_dev)

    own_bc = lax.dynamic_slice_in_dim(bc_load, team * quarter, quarter)
    small = jnp.concatenate([dt_load.T, doc_ids.astype(BF16)[None]], axis=0)
    extra = small.size // 256
    fill = jnp.zeros((-extra % 16, 256), BF16)
    held = jnp.concatenate([own_bc, small.reshape(-1, 256), fill], axis=0)[None]
    came, reach = [me], shards // 2
    while reach >= 1:
        held = jnp.concatenate([held, ring(held, reach)], axis=0)
        came = came + [t ^ reach for t in came]
        reach //= 2
    came = jnp.stack(came)
    part_bc = held[:, :quarter].reshape(shards * quarter, 256)
    small = jnp.take(held[:, quarter : quarter + extra], inverse(came), axis=0)
    small = small.reshape(shards, heads_dev + 1, rows_dev)
    docs = small[:, heads_dev].astype(F32).reshape(tokens)
    dt_all = lax.dynamic_slice_in_dim(small, me * width // head_dim, heads, axis=1)
    pieces, order, reach = [part_bc], [team], teams // 2
    while reach >= 1:
        pieces = pieces + [across(v, reach) for v in pieces]
        order = order + [t ^ reach for t in order]
        reach //= 2
    order = jnp.stack(order)
    dest_bc = jnp.take(destination.reshape(shards, teams, quarter), order, axis=1)
    dest_bc = jnp.take(dest_bc, came, axis=0).transpose(1, 0, 2).reshape(1, tokens)
    dt_bc = jnp.take(dt_all.reshape(shards, heads, teams, quarter), order, axis=2)
    dt_bc = jnp.take(dt_bc, came, axis=0).transpose(1, 2, 0, 3).reshape(heads, tokens)
    dt_bc = jnp.concatenate([dt_bc, jnp.zeros((16 - heads, tokens), BF16)], axis=0)

    rate_here = lax.dynamic_slice_in_dim(decay_rate, me * width // head_dim, heads)
    rate_row = jnp.repeat(rate_here, width // heads)[None]
    rate_lane = jnp.concatenate([rate_here, jnp.zeros((128 - heads,), F32)])[None]

    x_all = exchange(by_channel(x_load))
    bc_ctx, dt_ctx = place(dest_bc, dt_bc, pieces, width, head_dim)
    dy_all = exchange(after(by_channel(grad_y), x_all))
    y_sent, y_all, x_ctx, states = fore(docs, destination, x_all, rate_row, bc_ctx, dt_ctx)
    y_got = exchange(after(y_sent, dy_all))
    dx_ctx, keep, give, ddt_ctx = back(
        docs, (team % 2)[None], rate_row, rate_lane, bc_ctx, dt_ctx, x_ctx, dy_all, y_all,
        states, head_dim,
    )
    more = across(give, 1)
    dx_sent = gather_back(destination, dx_ctx, shards)
    dx_got = exchange(after(dx_sent, y_got))
    cbits, hbits = shards.bit_length() - 1, teams.bit_length() - 1
    near = [("ctx", 1 << k) for k in reversed(range(cbits))]
    links = near + [("head", 1 << k) for k in reversed(range(1, hbits))]
    turns = sorted(links, key=lambda v: (v[0] == "ctx", v[1]))

    def bit_of(axis, reach):
        return (lax.axis_index(axis) // reach) % 2

    def swap(v, axis, reach):
        return lax.ppermute(v, axis, [(i, i ^ reach) for i in range(lax.axis_size(axis))])

    axis, reach = turns[0]
    at = links.index(turns[0])
    links.pop(at)
    spots = destination.reshape((2,) * (cbits + hbits - 1) + (2 * quarter,))
    bit = bit_of(axis, reach)
    kept_spots = lax.dynamic_index_in_dim(spots, bit, at, False)
    given_spots = lax.dynamic_index_in_dim(spots, 1 - bit, at, False)
    given = gather_rows(given_spots.reshape(-1), keep, more)
    came = swap(given, axis, reach)
    kept = gather_rows(kept_spots.reshape(-1), keep, more)
    part = (kept + came).reshape(kept_spots.shape + (128,))
    for axis, reach in turns[1:]:
        at = links.index((axis, reach))
        links.pop(at)
        bit = bit_of(axis, reach)
        give = lax.dynamic_index_in_dim(part, 1 - bit, at, False)
        part = lax.dynamic_index_in_dim(part, bit, at, False) + swap(give, axis, reach)
    part = part.astype(BF16)
    for reach in (1 << k for k in range(hbits)):
        other, first = across(part, reach), bit_of("head", reach) == 0
        low, high = jnp.where(first, part, other), jnp.where(first, other, part)
        part = jnp.concatenate([low, high], axis=1 if reach == 1 else 0)
    dbc_load = part

    ddt = gather_turn(destination, ddt_ctx, heads)[:heads]
    ddt = ddt.reshape(heads, shards, rows_dev).transpose(1, 0, 2)
    ddt = ddt if sharing > 1 else ddt.astype(BF16)
    ddt = ddt.reshape((2,) * cbits + (heads, rows_dev))
    for at, (axis, reach) in enumerate(near):
        bit = bit_of(axis, reach)
        stay = lax.dynamic_index_in_dim(ddt, bit, at, True)
        came = swap(lax.dynamic_index_in_dim(ddt, 1 - bit, at, True), axis, reach)
        low, high = jnp.where(bit == 0, stay, came), jnp.where(bit == 0, came, stay)
        ddt = jnp.concatenate([low, high], axis=at)
    ddt = jnp.sum(ddt.astype(F32).reshape(heads_dev, sharing, rows_dev), axis=1)
    return (from_channel(y_got), from_channel(dx_got), dbc_load, ddt.T.astype(BF16))


def inverse(order):
    teams = jnp.arange(order.shape[0], dtype=order.dtype)
    return jnp.argmax(order[None, :] == teams[:, None], axis=1)


def solution(mesh):
    return jax.shard_map(
        body,
        mesh=mesh,
        in_specs=(
            P("ctx", "head"),
            P("ctx", None),
            P("ctx", "head"),
            P("head"),
            P("ctx"),
            P(),
            P("ctx", "head"),
        ),
        out_specs=(P("ctx", "head"), P("ctx", "head"), P("ctx", None), P("ctx", "head")),
        check_vma=False,
    )
```

time: 399 us -> 332 us (0.83)
  blocking collectives: 41.9 us -> 0 us
  waiting for transfers between devices: 168 us -> 149 us
  Pallas kernels: 126 us -> 108 us
  local copies, waits for them, and re-layouts: 18.8 us -> 30.3 us
    all_to_all x6 -> x4, waiting for transfers between devices: 125 us -> 36.4 us  [exchange(): return lax.all_to_all(v, 'ctx', split_axis=0, concat_axis=0, tiled=True)]
    ppermute x8 -> x16, waiting for transfers between devices: 42.9 us -> 113 us  [the longest x3 65.2 us: ring(): return lax.ppermute(v, 'ctx', [(i, i ^ reach) for i in range(shards)])]
    all_to_all x2 -> x0, blocking collectives: 41.9 us -> none  [exchange(): return lax.all_to_all(v, 'ctx', split_axis=0, concat_axis=0, tiled=True)]
    pallas_call x3 -> x7, Pallas kernels: 126 us -> 108 us  [the longest x1 28.1 us: back(): pl.pallas_call(functools.partial(back_kernel, blocks, head_dim), grid=(bl...]
    ppermute x8 -> x16, starting transfers between devices: 5.9 us -> 14.9 us  [the longest x7 6.6 us: swap(): lax.ppermute(v, axis, [(i, i ^ reach) for i in range(lax.axis_size(axis))])]
    unnamed x18 -> x28, local copies, waits for them, and re-layouts: 1.38 us -> 9.07 us
    all_to_all x6 -> x4, starting transfers between devices: 27.3 us -> 21.9 us  [exchange(): return lax.all_to_all(v, 'ctx', split_axis=0, concat_axis=0, tiled=True)]
  transfers between devices with their start and end apart: 14 -> 20, of which waited for: 8 -> 12; matrix products, arithmetic and copies ran while one was open for 5% -> 9% of each run, Pallas kernels for 15% -> 20%
where the time goes in v2:
time: 332 us
  waiting for transfers between devices  149 us (45%)
  Pallas kernels  108 us (33%)
  starting transfers between devices  36.7 us (11%)
  local copies, waits for them, and re-layouts  30.3 us (9%)
  other arithmetic  6.03 us (2%)
    ppermute x3, waiting for transfers between devices, ring(): return lax.ppermute(v, 'ctx', [(i, i ^ reach) for i in range(shards)])  65.2 us
    ppermute x7, waiting for transfers between devices, swap(): lax.ppermute(v, axis, [(i, i ^ reach) for i in range(lax.axis_size(axis))])  40.1 us
    all_to_all x4, waiting for transfers between devices, exchange(): return lax.all_to_all(v, 'ctx', split_axis=0, concat_axis=0, tiled=True)  36.4 us
    pallas_call x1, Pallas kernels, back(): pl.pallas_call(functools.partial(back_kernel, blocks, head_dim), grid=(bl...  28.1 us
    pallas_call x1, Pallas kernels, fore(): pl.pallas_call(fore_kernel, grid=(blocks,), in_specs=[SMEM, rowed(1, same...  26.2 us
    all_to_all x4, starting transfers between devices, exchange(): return lax.all_to_all(v, 'ctx', split_axis=0, concat_axis=0, tiled=True)  21.9 us
    pallas_call x1, Pallas kernels, place(): pl.pallas_call(functools.partial(place_kernel, len(pieces), head_dim), gr...  21.1 us
    pallas_call x1, Pallas kernels, gather_back(): pl.pallas_call(gather_kernel, grid=(shards,), in_specs=[blocked(1, lambda...  12.8 us
  transfers between devices with their start and end apart: 20, of which 12 were waited for; matrix products, arithmetic and copies ran while one was open for 9% of the time, Pallas kernels for 20%

profile of v2, /device:TPU:0, one launch (start us, length us, event | category | flops | bytes accessed | tf_op | source)
XLA Modules:
  0.0 331.5 jit_solution(16133578184130759393)
XLA Ops:
  0.6 3.1 copy.74
  3.7 7.4 %all-to-all-start = ((bf16[8,512,256]{2,1,0:T(8,128)(2,1)}), bf16[8,512,256]{2,1,0:T(8,128)(2,1)}, u32[]{:S(2)}, u32[]{:S(2)}) async-start(bf16[8,512,256]{2,1,0:T(8,128)(2,1)} %bitcast.112), calls=%async_computation | async-start | bytes 4194304 | tf_op jit(solution)/shard_map/all_to_all | solution.py:374
  11.4 3.0 collective-permute-start
  15.3 0.6 iota_reduce_fusion
  16.1 2.9 copy.52
  19.0 2.4 copy.53
  21.4 42.6 %collective-permute-done = bf16[1,208,256]{2,1,0:T(8,128)(2,1)S(1)} collective-permute-done((bf16[1,208,256]{2,1,0:T(8,128)(2,1)S(1)}, bf16[1,208,256]{2,1,0:T(8,128)(2,1)S(1)}, u32[]{:S(2)}, u32[]{:S(2)}) %collective-permute-start) | collective-permute-done | bytes 106528 | tf_op jit(solution)/shard_map/ppermute | solution.py:377
  64.7 5.3 %collective-permute-done.1 = bf16[2,208,256]{2,1,0:T(8,128)(2,1)S(1)} collective-permute-done((bf16[2,208,256]{2,1,0:T(8,128)(2,1)S(1)}, bf16[2,208,256]{2,1,0:T(8,128)(2,1)S(1)}, u32[]{:S(2)}, u32[]{:S(2)}) %collective-permute-start.1) | collective-permute-done | bytes 213024 | tf_op jit(solution)/shard_map/ppermute | solution.py:377
  70.1 1.8 collective-permute-start.2
  72.0 4.5 %all-to-all-start.1 = ((bf16[8,512,256]{2,1,0:T(8,128)(2,1)}), bf16[8,512,256]{2,1,0:T(8,128)(2,1)S(1)}, u32[]{:S(2)}, u32[]{:S(2)}) async-start(bf16[8,512,256]{2,1,0:T(8,128)(2,1)} %bitcast.43), calls=%async_computation.1 | async-start | bytes 4194304 | tf_op jit(solution)/shard_map/all_to_all | solution.py:374
  76.5 17.3 %collective-permute-done.2 = bf16[4,208,256]{2,1,0:T(8,128)(2,1)S(1)} collective-permute-done((bf16[4,208,256]{2,1,0:T(8,128)(2,1)S(1)}, bf16[4,208,256]{2,1,0:T(8,128)(2,1)S(1)}, u32[]{:S(2)}, u32[]{:S(2)}) %collective-permute-start.2) | collective-permute-done | bytes 426016 | tf_op jit(solution)/shard_map/ppermute | solution.py:377
  93.7 0.9 pad_maximum_fusion
  94.6 1.5 collective-permute-start.3
  98.0 2.0 copy.56.dest_col
  101.3 2.7 collective-permute-done.3.refs_1_
  104.9 0.7 concatenate.85.dt_ref
  105.6 2.0 copy.67
  108.2 0.8 copy-done.9
  109.0 21.1 %place.1 = (bf16[4096,256]{1,0:T(8,128)(2,1)}, bf16[4096,256]{1,0:T(8,128)(2,1)}) custom-call(s32[1,4096]{1,0:T(1,128)} %bitcast.146, bf16[16,4096]{1,0:T(8,128)(2,1)} %concatenate.85.dt_ref, bf16[1024,256]{1,0:T(8,128)(2,1)} %bitcast.39.refs_0_, bf16[1024,256]{1,0:T(8,128)(2,1)} %collective-permute-done.3.refs_1_, ...), custom_call_target="tpu_custom_call" | custom-call | flops 12884901888 | bytes 6553600 | tf_op jit(solution)/shard_map/place/pallas_call | solution.py:231
  130.2 26.2 %fore.1 = (bf16[4096,256]{1,0:T(8,128)(2,1)}, f32[4096,256]{1,0:T(8,128)}, bf16[4096,256]{1,0:T(8,128)(2,1)}, f32[16,128,256]{2,1,0:T(8,128)}) custom-call(f32[4096]{0:T(1024)} %bitcast.147, f32[1,4096]{1,0:T(1,128)} %bitcast.140, f32[4096,1]{1,0:T(8,128)} %bitcast.125, s32[1,4096]{1,0:T(1,128)} %bitcast.130, bf16[4096,256]{1,0:T(8,128)(2,1)} %bitcast.13.x_ref, ...), custom_call_target="tpu_custom_call" | custom-call | flops 12784238592 | bytes 16384000 | tf_op jit(solution)/shard_map/fore/pallas_call | solution.py:249
  156.4 1.4 copy-done.3
  157.8 28.1 %back.1 = (bf16[4096,256]{1,0:T(8,128)(2,1)}, f32[4096,128]{1,0:T(8,128)}, f32[4096,128]{1,0:T(8,128)}, f32[4096,128]{1,0:T(8,128)}) custom-call(f32[4096]{0:T(1024)} %bitcast.148, s32[1]{0:T(128)} %bitcast.48.side_smem, f32[1,4096]{1,0:T(1,128)} %bitcast.141, f32[4096,1]{1,0:T(8,128)} %bitcast.126, f32[1,256]{1,0:T(1,128)} %broadcast_in_dim_reshape.2.rate_ref, ...), custom_call_target="tpu_custom_call" | custom-call | flops 8388608000 | bytes 24576000 | tf_op jit(solution)/shard_map/back/pallas_call | solution.py:278
  185.8 12.8 %gather_back.1 = bf16[4096,256]{1,0:T(8,128)(2,1)} custom-call(s32[4096,1]{1,0:T(8,128)} %copy.56.dest_col, bf16[4096,256]{1,0:T(8,128)(2,1)} %get-tuple-element.26.dx_ref), custom_call_target="tpu_custom_call" | custom-call | flops 8589934592 | bytes 6144000 | tf_op jit(solution)/shard_map/gather_back/pallas_call | solution.py:343
  198.7 6.4 %all-to-all-start.3 = ((bf16[8,512,256]{2,1,0:T(8,128)(2,1)}), bf16[8,512,256]{2,1,0:T(8,128)(2,1)}, u32[]{:S(2)}, u32[]{:S(2)}) async-start(bf16[8,512,256]{2,1,0:T(8,128)(2,1)} %bitcast.124), calls=%async_computation.3 | async-start | bytes 4194304 | tf_op jit(solution)/shard_map/all_to_all | solution.py:374
  205.9 3.5 %collective-permute-done.6.more_ref = f32[4096,128]{1,0:T(8,128)S(1)} collective-permute-done((f32[4096,128]{1,0:T(8,128)}, f32[4096,128]{1,0:T(8,128)S(1)}, u32[]{:S(2)}, u32[]{:S(2)}) %collective-permute-start.6) | collective-permute-done | bytes 2097184 | tf_op jit(solution)/shard_map/ppermute | solution.py:380
  209.4 1.3 copy-done.2
  210.7 5.4 %gather_rows.3 = f32[2048,128]{1,0:T(8,128)} custom-call(s32[2048]{0:T(1024)} %bitcast.143, f32[4096,128]{1,0:T(8,128)} %get-tuple-element.27.keep_ref, f32[4096,128]{1,0:T(8,128)} %copy-done.2), custom_call_target="tpu_custom_call" | custom-call | flops 524288 | bytes 6291456 | tf_op jit(solution)/shard_map/gather_rows/pallas_call | solution.py:308
  216.1 1.5 collective-permute-start.7
  217.6 36.4 %all-to-all-done.3 = bf16[8,512,256]{2,1,0:T(8,128)(2,1)} async-done(((bf16[8,512,256]{2,1,0:T(8,128)(2,1)}), bf16[8,512,256]{2,1,0:T(8,128)(2,1)}, u32[]{:S(2)}, u32[]{:S(2)}) %all-to-all-start.3) | async-done | bytes 2097184 | tf_op jit(solution)/shard_map/all_to_all | solution.py:374
  254.0 3.6 %all-to-all-start.2 = ((bf16[8,512,256]{2,1,0:T(8,128)(2,1)}), bf16[8,512,256]{2,1,0:T(8,128)(2,1)S(1)}, u32[]{:S(2)}, u32[]{:S(2)}) async-start(bf16[8,512,256]{2,1,0:T(8,128)(2,1)} %bitcast.122), calls=%async_computation.2 | async-start | bytes 4194304 | tf_op jit(solution)/shard_map/all_to_all | solution.py:374
  257.7 5.4 %gather_rows.2 = f32[2048,128]{1,0:T(8,128)} custom-call(s32[2048]{0:T(1024)} %bitcast.142, f32[4096,128]{1,0:T(8,128)} %get-tuple-element.27.keep_ref, f32[4096,128]{1,0:T(8,128)} %copy-done.2), custom_call_target="tpu_custom_call" | custom-call | flops 524288 | bytes 6291456 | tf_op jit(solution)/shard_map/gather_rows/pallas_call | solution.py:308
  263.0 1.6 add.143
  264.7 0.8 dynamic-slice_bitcast_fusion
  265.5 2.0 collective-permute-start.8
  267.5 9.3 %gather_turn.1 = f32[8,4096]{1,0:T(8,128)} custom-call(s32[4096]{0:T(1024)} %dest_smem.1, f32[4096,128]{1,0:T(8,128)} %get-tuple-element.29.ddt_ref), custom_call_target="tpu_custom_call" | custom-call | flops 1048576 | bytes 4096000 | tf_op jit(solution)/shard_map/gather_turn/pallas_call | solution.py:325
  276.9 0.9 slice.32
  277.9 2.4 collective-permute-start.13
  280.3 14.2 %collective-permute-done.8 = f32[2,2,256,128]{3,2,1,0:T(8,128)} collective-permute-done((f32[2,2,256,128]{3,2,1,0:T(8,128)}, f32[2,2,256,128]{3,2,1,0:T(8,128)}, u32[]{:S(2)}, u32[]{:S(2)}) %collective-permute-start.8) | collective-permute-done | bytes 524320 | tf_op jit(solution)/shard_map/ppermute | solution.py:443
  294.5 1.1 bitcast_add_fusion
  295.7 11.2 %collective-permute-done.13 = bf16[1,2,2,4,512]{4,3,2,1,0:T(4,128)(2,1)S(1)} collective-permute-done((bf16[1,2,2,4,512]{4,3,2,1,0:T(4,128)(2,1)S(1)}, bf16[1,2,2,4,512]{4,3,2,1,0:T(4,128)(2,1)S(1)}, u32[]{:S(2)}, u32[]{:S(2)}) %collective-permute-start.13) | collective-permute-done | bytes 16416 | tf_op jit(solution)/shard_map/ppermute | solution.py:443
  307.1 5.5 %collective-permute-done.9 = f32[2,256,128]{2,1,0:T(8,128)S(1)} collective-permute-done((f32[2,256,128]{2,1,0:T(8,128)S(1)}, f32[2,256,128]{2,1,0:T(8,128)S(1)}, u32[]{:S(2)}, u32[]{:S(2)}) %collective-permute-start.9) | collective-permute-done | bytes 262176 | tf_op jit(solution)/shard_map/ppermute | solution.py:443
  313.0 8.3 %collective-permute-done.10 = f32[256,128]{1,0:T(8,128)S(1)} collective-permute-done((f32[256,128]{1,0:T(8,128)S(1)}, f32[256,128]{1,0:T(8,128)S(1)}, u32[]{:S(2)}, u32[]{:S(2)}) %collective-permute-start.10) | collective-permute-done | bytes 131104 | tf_op jit(solution)/shard_map/ppermute | solution.py:443
  321.5 1.1 collective-permute-done.11
  322.7 1.6 collective-permute-start.12
  324.3 1.0 collective-permute-done.15
  326.0 3.2 copy.63
  329.1 1.6 copy.62
  330.8 0.7 pad_maximum_fusion.5
  (101 shorter events, 9.3 us)
Async XLA Ops:
  0.6 10.7 %copy-start = (bf16[512,256]{1,0:T(8,128)(2,1)S(1)}, bf16[512,256]{1,0:T(8,128)(2,1)}, u32[]{:S(2)}) copy-start(bf16[512,256]{1,0:T(8,128)(2,1)} %param.8) | copy-start | bytes 786436
  3.7 7.4 %copy-start.8 = (s32[512]{0:T(512)S(1)}, s32[512]{0:T(512)}, u32[]{:S(2)}) copy-start(s32[512]{0:T(512)} %param.11) | copy-start | bytes 6148
  3.7 7.4 %copy-start.7 = (bf16[512,32]{0,1:T(8,128)(2,1)S(1)}, bf16[512,32]{0,1:T(8,128)(2,1)}, u32[]{:S(2)}) copy-start(bf16[512,32]{0,1:T(8,128)(2,1)} %param.9) | copy-start | bytes 98308
  3.7 10.7 %copy-start.4 = (s32[4096]{0:T(1024)S(1)}, s32[4096]{0:T(1024)}, u32[]{:S(2)}) copy-start(s32[4096]{0:T(1024)} %dest_smem.1) | copy-start | bytes 49156
  3.7 68.2 %all-to-all-start = ((bf16[8,512,256]{2,1,0:T(8,128)(2,1)}), bf16[8,512,256]{2,1,0:T(8,128)(2,1)}, u32[]{:S(2)}, u32[]{:S(2)}) async-start(bf16[8,512,256]{2,1,0:T(8,128)(2,1)} %bitcast.112), calls=%async_computation | async-start | bytes 4194304 | tf_op jit(solution)/shard_map/all_to_all | solution.py:374
  11.4 52.5 %collective-permute-start = (bf16[1,208,256]{2,1,0:T(8,128)(2,1)S(1)}, bf16[1,208,256]{2,1,0:T(8,128)(2,1)S(1)}, u32[]{:S(2)}, u32[]{:S(2)}) collective-permute-start(bf16[1,208,256]{2,1,0:T(8,128)(2,1)S(1)} %maximum_bitcast_fusion), channel_id=1, source_target_pairs={{0,16},{4,20},{8,24},{12,28},{16,0},{20,4},{24,8},{28,12},{1,17},{... | collective-permute-start | bytes 319496 | tf_op jit(solution)/shard_map/ppermute | solution.py:377
  18.9 45.7 %copy-start.10 = (f32[32]{0:T(128)S(1)}, f32[32]{0:T(128)}, u32[]{:S(2)}) copy-start(f32[32]{0:T(128)} %param.10) | copy-start | bytes 388
  64.0 6.1 %collective-permute-start.1 = (bf16[2,208,256]{2,1,0:T(8,128)(2,1)S(1)}, bf16[2,208,256]{2,1,0:T(8,128)(2,1)S(1)}, u32[]{:S(2)}, u32[]{:S(2)}) collective-permute-start(bf16[2,208,256]{2,1,0:T(8,128)(2,1)S(1)} %pad_maximum_fusion.6), channel_id=1, source_target_pairs={{0,8},{4,12},{8,0},{12,4},{16,24},{20,28},{24,16},{28,20},{1,9},{5... | collective-permute-start | bytes 638984 | tf_op jit(solution)/shard_map/ppermute | solution.py:377
  70.1 23.6 %collective-permute-start.2 = (bf16[4,208,256]{2,1,0:T(8,128)(2,1)S(1)}, bf16[4,208,256]{2,1,0:T(8,128)(2,1)S(1)}, u32[]{:S(2)}, u32[]{:S(2)}) collective-permute-start(bf16[4,208,256]{2,1,0:T(8,128)(2,1)S(1)} %pad_maximum_fusion.3), channel_id=1, source_target_pairs={{0,4},{4,0},{8,12},{12,8},{16,20},{20,16},{24,28},{28,24},{1,5},{5... | collective-permute-start | bytes 1277960 | tf_op jit(solution)/shard_map/ppermute | solution.py:377
  72.0 84.4 %all-to-all-start.1 = ((bf16[8,512,256]{2,1,0:T(8,128)(2,1)}), bf16[8,512,256]{2,1,0:T(8,128)(2,1)S(1)}, u32[]{:S(2)}, u32[]{:S(2)}) async-start(bf16[8,512,256]{2,1,0:T(8,128)(2,1)} %bitcast.43), calls=%async_computation.1 | async-start | bytes 4194304 | tf_op jit(solution)/shard_map/all_to_all | solution.py:374
  94.6 9.5 %collective-permute-start.3 = (bf16[1024,256]{1,0:T(8,128)(2,1)}, bf16[1024,256]{1,0:T(8,128)(2,1)}, u32[]{:S(2)}, u32[]{:S(2)}) collective-permute-start(bf16[1024,256]{1,0:T(8,128)(2,1)} %bitcast.39.refs_0_), channel_id=1, source_target_pairs={{0,2},{1,3},{2,0},{3,1},{4,6},{5,7},{6,4},{7,5},{8,10},{9,11},{10,... | collective-permute-start | bytes 1572872 | tf_op jit(solution)/shard_map/ppermute | solution.py:380
  100.0 8.2 %collective-permute-start.4 = (bf16[1024,256]{1,0:T(8,128)(2,1)}, bf16[1024,256]{1,0:T(8,128)(2,1)}, u32[]{:S(2)}, u32[]{:S(2)}) collective-permute-start(bf16[1024,256]{1,0:T(8,128)(2,1)} %bitcast.39.refs_0_), channel_id=1, source_target_pairs={{0,1},{1,0},{2,3},{3,2},{4,5},{5,4},{6,7},{7,6},{8,9},{9,8},{10,11... | collective-permute-start | bytes 1572872 | tf_op jit(solution)/shard_map/ppermute | solution.py:380
  104.1 4.1 %collective-permute-start.5 = (bf16[1024,256]{1,0:T(8,128)(2,1)}, bf16[1024,256]{1,0:T(8,128)(2,1)S(1)}, u32[]{:S(2)}, u32[]{:S(2)}) collective-permute-start(bf16[1024,256]{1,0:T(8,128)(2,1)} %collective-permute-done.3.refs_1_), channel_id=1, source_target_pairs={{0,1},{1,0},{2,3},{3,2},{4,5},{5,4},{6,7},{7,6},{8,9},{9,8},{10,11... | collective-permute-start | bytes 1572872 | tf_op jit(solution)/shard_map/ppermute | solution.py:380
  105.6 24.5 %copy-start.6 = (f32[1,1,8,512]{3,1,2,0:T(1,128)}, f32[1,1,8,512]{3,1,2,0:T(1,128)S(1)}, u32[]{:S(2)}) copy-start(f32[1,1,8,512]{3,1,2,0:T(1,128)S(1)} %copy.65) | copy-start | bytes 49156
  108.2 0.8 copy-start.9
  156.4 1.4 copy-start.3
  198.7 6.6 %copy-start.5 = (s32[4096]{0:T(1024)S(1)}, s32[4096]{0:T(1024)}, u32[]{:S(2)}) copy-start(s32[4096]{0:T(1024)} %dest_smem.1) | copy-start | bytes 49156
  198.7 55.4 %all-to-all-start.3 = ((bf16[8,512,256]{2,1,0:T(8,128)(2,1)}), bf16[8,512,256]{2,1,0:T(8,128)(2,1)}, u32[]{:S(2)}, u32[]{:S(2)}) async-start(bf16[8,512,256]{2,1,0:T(8,128)(2,1)} %bitcast.124), calls=%async_computation.3 | async-start | bytes 4194304 | tf_op jit(solution)/shard_map/all_to_all | solution.py:374
  205.0 4.4 %collective-permute-start.6 = (f32[4096,128]{1,0:T(8,128)}, f32[4096,128]{1,0:T(8,128)S(1)}, u32[]{:S(2)}, u32[]{:S(2)}) collective-permute-start(f32[4096,128]{1,0:T(8,128)} %get-tuple-element.28), channel_id=1, source_target_pairs={{0,1},{1,0},{2,3},{3,2},{4,5},{5,4},{6,7},{7,6},{8,9},{9,8},{10,11... | collective-permute-start | bytes 6291464 | tf_op jit(solution)/shard_map/ppermute | solution.py:380
  209.4 1.3 copy-start.2
  216.1 46.9 %collective-permute-start.7 = (f32[2048,128]{1,0:T(8,128)}, f32[2048,128]{1,0:T(8,128)}, u32[]{:S(2)}, u32[]{:S(2)}) collective-permute-start(f32[2048,128]{1,0:T(8,128)} %gather_rows.3), channel_id=1, source_target_pairs={{0,2},{1,3},{2,0},{3,1},{4,6},{5,7},{6,4},{7,5},{8,10},{9,11},{10,... | collective-permute-start | bytes 3145736 | tf_op jit(solution)/shard_map/ppermute | solution.py:443
  254.0 75.1 %all-to-all-start.2 = ((bf16[8,512,256]{2,1,0:T(8,128)(2,1)}), bf16[8,512,256]{2,1,0:T(8,128)(2,1)S(1)}, u32[]{:S(2)}, u32[]{:S(2)}) async-start(bf16[8,512,256]{2,1,0:T(8,128)(2,1)} %bitcast.122), calls=%async_computation.2 | async-start | bytes 4194304 | tf_op jit(solution)/shard_map/all_to_all | solution.py:374
  265.5 29.0 %collective-permute-start.8 = (f32[2,2,256,128]{3,2,1,0:T(8,128)}, f32[2,2,256,128]{3,2,1,0:T(8,128)}, u32[]{:S(2)}, u32[]{:S(2)}) collective-permute-start(f32[2,2,256,128]{3,2,1,0:T(8,128)} %dynamic-slice_bitcast_fusion), channel_id=1, source_target_pairs={{0,4},{4,0},{8,12},{12,8},{16,20},{20,16},{24,28},{28,24},{1,5},{5... | collective-permute-start | bytes 1572872 | tf_op jit(solution)/shard_map/ppermute | solution.py:443
  277.9 29.0 %collective-permute-start.13 = (bf16[1,2,2,4,512]{4,3,2,1,0:T(4,128)(2,1)S(1)}, bf16[1,2,2,4,512]{4,3,2,1,0:T(4,128)(2,1)S(1)}, u32[]{:S(2)}, u32[]{:S(2)}) collective-permute-start(bf16[1,2,2,4,512]{4,3,2,1,0:T(4,128)(2,1)S(1)} %constant_dynamic-slice_fusion), channel_id=1, source_target_pairs={{0,16},{4,20},{8,24},{12,28},{16,0},{20,4},{24,8},{28,12},{1,17},{... | collective-permute-start | bytes 49160 | tf_op jit(solution)/shard_map/ppermute | solution.py:443
  295.6 16.9 %collective-permute-start.9 = (f32[2,256,128]{2,1,0:T(8,128)S(1)}, f32[2,256,128]{2,1,0:T(8,128)S(1)}, u32[]{:S(2)}, u32[]{:S(2)}) collective-permute-start(f32[2,256,128]{2,1,0:T(8,128)S(1)} %dynamic-slice_bitcast_fusion.1), channel_id=1, source_target_pairs={{0,8},{4,12},{8,0},{12,4},{16,24},{20,28},{24,16},{28,20},{1,9},{5... | collective-permute-start | bytes 786440 | tf_op jit(solution)/shard_map/ppermute | solution.py:443
  307.0 6.0 %collective-permute-start.14 = (bf16[2,1,2,4,512]{4,3,2,1,0:T(4,128)(2,1)S(1)}, bf16[2,1,2,4,512]{4,3,2,1,0:T(4,128)(2,1)S(1)}, u32[]{:S(2)}, u32[]{:S(2)}) collective-permute-start(bf16[2,1,2,4,512]{4,3,2,1,0:T(4,128)(2,1)S(1)} %fusion.3), channel_id=1, source_target_pairs={{0,8},{4,12},{8,0},{12,4},{16,24},{20,28},{24,16},{28,20},{1,9},{5... | collective-permute-start | bytes 49160 | tf_op jit(solution)/shard_map/ppermute | solution.py:443
  312.6 8.7 %collective-permute-start.10 = (f32[256,128]{1,0:T(8,128)S(1)}, f32[256,128]{1,0:T(8,128)S(1)}, u32[]{:S(2)}, u32[]{:S(2)}) collective-permute-start(f32[256,128]{1,0:T(8,128)S(1)} %dynamic-slice_bitcast_fusion.2), channel_id=1, source_target_pairs={{0,16},{4,20},{8,24},{12,28},{16,0},{20,4},{24,8},{28,12},{1,17},{... | collective-permute-start | bytes 393224 | tf_op jit(solution)/shard_map/ppermute | solution.py:443
  321.3 1.3 collective-permute-start.11
  321.5 3.8 %collective-permute-start.15 = (bf16[2,2,1,4,512]{4,3,2,1,0:T(4,128)(2,1)S(1)}, bf16[2,2,1,4,512]{4,3,2,1,0:T(4,128)(2,1)S(1)}, u32[]{:S(2)}, u32[]{:S(2)}) collective-permute-start(bf16[2,2,1,4,512]{4,3,2,1,0:T(4,128)(2,1)S(1)} %fusion.1), channel_id=1, source_target_pairs={{0,4},{4,0},{8,12},{12,8},{16,20},{20,16},{24,28},{28,24},{1,5},{5... | collective-permute-start | bytes 49160 | tf_op jit(solution)/shard_map/ppermute | solution.py:443
  322.7 8.0 %collective-permute-start.12 = (bf16[256,256]{1,0:T(8,128)(2,1)S(1)}, bf16[256,256]{1,0:T(8,128)(2,1)S(1)}, u32[]{:S(2)}, u32[]{:S(2)}) collective-permute-start(bf16[256,256]{1,0:T(8,128)(2,1)S(1)} %pad_maximum_fusion.7), channel_id=1, source_target_pairs={{0,2},{1,3},{2,0},{3,1},{4,6},{5,7},{6,4},{7,5},{8,10},{9,11},{10,... | collective-permute-start | bytes 393224 | tf_op jit(solution)/shard_map/ppermute | solution.py:380
  329.1 2.4 copy-start.1

commit v3 on v2

--- a/solution.py
+++ b/solution.py
@@ -120,12 +120,21 @@
 
 
 def back_kernel(
-    blocks, head_dim, doc_smem, side_smem, doc_ref, doc_col, rate_ref, rate_lane,
-    bc_ref, dt_ref, x_ref, dy_ref, y_ref, state_ref,
-    dx_out, keep_out, give_out, ddt_out,
-    grad_ref, sum_ref, lower_ref, spread_ref,
+    blocks, head_dim, pieces, slot_smem, doc_smem, side_smem, doc_ref, doc_col, rate_ref, rate_lane,
+    bc_ref, dt_ref, x_ref, y_ref, state_ref, *refs,
 ):
+    dy_refs = refs[:pieces]
+    dx_out, keep_out, give_out, ddt_out = refs[pieces : pieces + 4]
+    dy_ref, grad_ref, sum_ref, lower_ref, spread_ref = refs[pieces + 4 :]
     step = pl.program_id(0)
+    each = blocks // pieces
+    slot = slot_smem[(blocks - 1 - step) // each]
+    for e in range(pieces):
+
+        @pl.when(slot == e)
+        def _(e=e):
+            at = ((blocks - 1 - step) % each) * BLOCK
+            dy_ref[...] = dy_refs[e][pl.ds(pl.multiple_of(at, BLOCK), BLOCK), :]
 
     @pl.when(step == 0)
     def _():
@@ -214,15 +223,15 @@
 
 
 def blocked(cols, index, size=BLOCK):
-    return pl.BlockSpec((size, cols), lambda s: (index(s), 0))
+    return pl.BlockSpec((size, cols), lambda s, *more: (index(s), 0))
 
 
 def rowed(rows, index):
-    return pl.BlockSpec((rows, BLOCK), lambda s: (0, index(s)))
+    return pl.BlockSpec((rows, BLOCK), lambda s, *more: (0, index(s)))
 
 
 def planes(width, index):
-    return pl.BlockSpec((1, 128, width), lambda s: (index(s), 0, 0))
+    return pl.BlockSpec((1, 128, width), lambda s, *more: (index(s), 0, 0))
 
 
 def place(dest_bc, dt_bc, pieces, width, head_dim):
@@ -271,26 +280,30 @@
     )(docs, docs[None], docs[:, None], destination[None], x_all, rate_row, bc_ctx, dt_ctx)
 
 
-def back(docs, side, rate_row, rate_lane, bc_ctx, dt_ctx, x_ctx, dy_all, y_all, states, head_dim):
+def back(slots, docs, side, rate_row, rate_lane, bc_ctx, dt_ctx, x_ctx, dy_all, y_all, states, head_dim):
     tokens, width = x_ctx.shape
     blocks = tokens // BLOCK
     down = lambda s: blocks - 1 - s
     return pl.pallas_call(
-        functools.partial(back_kernel, blocks, head_dim),
-        grid=(blocks,),
-        in_specs=[
-            SMEM, SMEM, rowed(1, down), blocked(1, down), VMEM, VMEM,
-            blocked(256, down), blocked(width, down), blocked(width, down),
-            blocked(width, down), blocked(width, down), planes(width, down),
-        ],
-        out_specs=[blocked(width, down)] + [blocked(128, down)] * 3,
+        functools.partial(back_kernel, blocks, head_dim, len(dy_all)),
+        grid_spec=pltpu.PrefetchScalarGridSpec(
+            num_scalar_prefetch=1,
+            grid=(blocks,),
+            in_specs=[
+                SMEM, SMEM, rowed(1, down), blocked(1, down), VMEM, VMEM,
+                blocked(256, down), blocked(width, down), blocked(width, down),
+                blocked(width, down), planes(width, down),
+            ] + [VMEM] * len(dy_all),
+            out_specs=[blocked(width, down)] + [blocked(128, down)] * 3,
+            scratch_shapes=[
+                pltpu.VMEM((BLOCK, width), BF16),
+                pltpu.VMEM((128, width), F32),
+                pltpu.VMEM((8, 128), F32),
+                pltpu.VMEM((BLOCK, BLOCK), BF16),
+                pltpu.VMEM((2 * width, 128), BF16),
+            ],
+        ),
         out_shape=[struct(BF16, tokens, width)] + [struct(F32, tokens, 128)] * 3,
-        scratch_shapes=[
-            pltpu.VMEM((128, width), F32),
-            pltpu.VMEM((8, 128), F32),
-            pltpu.VMEM((BLOCK, BLOCK), BF16),
-            pltpu.VMEM((2 * width, 128), BF16),
-        ],
         compiler_params=params(),
         cost_estimate=pl.CostEstimate(
             flops=2 * tokens * 4000 * width,
@@ -299,8 +312,8 @@
         ),
         name="back",
     )(
-        docs, side, docs[None], docs[:, None], rate_row, rate_lane,
-        bc_ctx, dt_ctx, x_ctx, dy_all, y_all, states,
+        slots, docs, side, docs[None], docs[:, None], rate_row, rate_lane,
+        bc_ctx, dt_ctx, x_ctx, y_all, states, *dy_all,
     )
 
 
@@ -392,10 +405,11 @@
     extra = small.size // 256
     fill = jnp.zeros((-extra % 16, 256), BF16)
     held = jnp.concatenate([own_bc, small.reshape(-1, 256), fill], axis=0)[None]
-    came, reach = [me], shards // 2
+    came, reach, early = [me], shards // 2, None
     while reach >= 1:
         held = jnp.concatenate([held, ring(held, reach)], axis=0)
         came = came + [t ^ reach for t in came]
+        early = held if reach > 1 else early
         reach //= 2
     came = jnp.stack(came)
     part_bc = held[:, :quarter].reshape(shards * quarter, 256)
@@ -421,11 +435,17 @@
 
     x_all = exchange(by_channel(x_load))
     bc_ctx, dt_ctx = place(dest_bc, dt_bc, pieces, width, head_dim)
-    dy_all = exchange(after(by_channel(grad_y), x_all))
+    slots = jnp.arange(shards, dtype=I32) ^ me
+    parts = grad_y.reshape(rows_dev, shards, width).transpose(1, 0, 2)
+    late = me + jnp.where(early[-1, quarter + extra - 1, -1] < 0, 1, 0)
+    dy_all = []
+    for e in range(shards):
+        piece = lax.dynamic_index_in_dim(parts, late ^ e, 0, False)
+        dy_all.append(ring(piece, e) if e else piece)
     y_sent, y_all, x_ctx, states = fore(docs, destination, x_all, rate_row, bc_ctx, dt_ctx)
-    y_got = exchange(after(y_sent, dy_all))
+    y_got = exchange(y_sent)
     dx_ctx, keep, give, ddt_ctx = back(
-        docs, (team % 2)[None], rate_row, rate_lane, bc_ctx, dt_ctx, x_ctx, dy_all, y_all,
+        slots, docs, (team % 2)[None], rate_row, rate_lane, bc_ctx, dt_ctx, x_ctx, dy_all, y_all,
         states, head_dim,
     )
     more = across(give, 1)

time: 332 us -> 315 us (0.949)
  waiting for transfers between devices: 149 us -> 119 us
  local copies, waits for them, and re-layouts: 30.3 us -> 34.2 us
  starting transfers between devices: 36.7 us -> 40.5 us
    ppermute x3 -> x10, waiting for transfers between devices: 65.2 us -> 36.9 us  [ring(): return lax.ppermute(v, 'ctx', [(i, i ^ reach) for i in range(shards)])]
    ppermute x3 -> x10, starting transfers between devices: 4.84 us -> 19.5 us  [ring(): return lax.ppermute(v, 'ctx', [(i, i ^ reach) for i in range(shards)])]
    all_to_all x4 -> x3, starting transfers between devices: 21.9 us -> 12.6 us  [exchange(): return lax.all_to_all(v, 'ctx', split_axis=0, concat_axis=0, tiled=True)]
    another operation x0 -> x1, local copies, waits for them, and re-layouts: none -> 4.35 us
    unnamed x28 -> x40, local copies, waits for them, and re-layouts: 9.07 us -> 10.6 us
    all_to_all x4 -> x3, waiting for transfers between devices: 36.4 us -> 36.1 us  [exchange(): return lax.all_to_all(v, 'ctx', split_axis=0, concat_axis=0, tiled=True)]
  transfers between devices with their start and end apart: 20 -> 26, of which waited for: 12 -> 10; matrix products, arithmetic and copies ran while one was open for 9% -> 11% of each run, Pallas kernels for 20% -> 21%
where the time goes in v3:
time: 315 us; the launch traced here: 314 us
  waiting for transfers between devices  119 us (38%)
  Pallas kernels  111 us (35%)
  starting transfers between devices  40.5 us (13%)
  local copies, waits for them, and re-layouts  34.2 us (11%)
  other arithmetic  7.28 us (2%)
    ppermute x7, waiting for transfers between devices, swap(): lax.ppermute(v, axis, [(i, i ^ reach) for i in range(lax.axis_size(axis))])  41.1 us
    ppermute x10, waiting for transfers between devices, ring(): return lax.ppermute(v, 'ctx', [(i, i ^ reach) for i in range(shards)])  36.9 us
    all_to_all x3, waiting for transfers between devices, exchange(): return lax.all_to_all(v, 'ctx', split_axis=0, concat_axis=0, tiled=True)  36.1 us
    pallas_call x1, Pallas kernels, back(): pl.pallas_call(functools.partial(back_kernel, blocks, head_dim, len(dy_al...  30.8 us
    pallas_call x1, Pallas kernels, fore(): pl.pallas_call(fore_kernel, grid=(blocks,), in_specs=[SMEM, rowed(1, same...  26.2 us
    pallas_call x1, Pallas kernels, place(): pl.pallas_call(functools.partial(place_kernel, len(pieces), head_dim), gr...  21.1 us
    ppermute x10, starting transfers between devices, ring(): return lax.ppermute(v, 'ctx', [(i, i ^ reach) for i in range(shards)])  19.5 us
    pallas_call x1, Pallas kernels, gather_back(): pl.pallas_call(gather_kernel, grid=(shards,), in_specs=[blocked(1, lambda...  12.8 us
  transfers between devices with their start and end apart: 26, of which 10 were waited for; matrix products, arithmetic and copies ran while one was open for 11% of the time, Pallas kernels for 21%

profile of v3, /device:TPU:0, one launch (start us, length us, event | category | flops | bytes accessed | tf_op | source)
XLA Modules:
  0.0 314.0 jit_solution(5938076196048368251)
XLA Ops:
  1.4 0.8 pad_maximum_fusion.8
  2.4 4.1 %collective-permute-start = (bf16[1,208,256]{2,1,0:T(8,128)(2,1)S(1)}, bf16[1,208,256]{2,1,0:T(8,128)(2,1)S(1)}, u32[]{:S(2)}, u32[]{:S(2)}) collective-permute-start(bf16[1,208,256]{2,1,0:T(8,128)(2,1)S(1)} %maximum_bitcast_fusion), channel_id=1, source_target_pairs={{0,16},{4,20},{8,24},{12,28},{16,0},{20,4},{24,8},{28,12},{1,17},{... | collective-permute-start | bytes 319496 | tf_op jit(solution)/shard_map/ppermute | solution.py:390
  6.5 3.0 copy.119
  9.6 4.5 %all-to-all-start = ((bf16[8,512,256]{2,1,0:T(8,128)(2,1)}), bf16[8,512,256]{2,1,0:T(8,128)(2,1)}, u32[]{:S(2)}, u32[]{:S(2)}) async-start(bf16[8,512,256]{2,1,0:T(8,128)(2,1)} %bitcast.125), calls=%async_computation | async-start | bytes 4194304 | tf_op jit(solution)/shard_map/all_to_all | solution.py:387
  16.4 1.9 collective-permute-start.1
  18.4 2.3 copy.105
  22.1 2.0 copy.84.dest_col
  24.6 28.9 %collective-permute-done.1 = bf16[2,208,256]{2,1,0:T(8,128)(2,1)S(1)} collective-permute-done((bf16[2,208,256]{2,1,0:T(8,128)(2,1)S(1)}, bf16[2,208,256]{2,1,0:T(8,128)(2,1)S(1)}, u32[]{:S(2)}, u32[]{:S(2)}) %collective-permute-start.1) | collective-permute-done | bytes 213024 | tf_op jit(solution)/shard_map/ppermute | solution.py:390
  53.6 1.3 collective-permute-start.2
  56.7 8.0 %collective-permute-done.2 = bf16[4,208,256]{2,1,0:T(8,128)(2,1)S(1)} collective-permute-done((bf16[4,208,256]{2,1,0:T(8,128)(2,1)S(1)}, bf16[4,208,256]{2,1,0:T(8,128)(2,1)S(1)}, u32[]{:S(2)}, u32[]{:S(2)}) %collective-permute-start.2) | collective-permute-done | bytes 426016 | tf_op jit(solution)/shard_map/ppermute | solution.py:390
  64.7 1.6 collective-permute-start.3
  66.3 4.3 %constant_dynamic-slice_fusion.3 = (bf16[512,1,256]{2,1,0:T(2,128)(2,1)S(1)}, bf16[512,1,256]{2,1,0:T(2,128)(2,1)S(1)}, bf16[512,1,256]{2,1,0:T(2,128)(2,1)S(1)}...) fusion(bf16[512,8,256]{2,1,0:T(8,128)(2,1)S(1)} %bitcast.138, ...), kind=kLoop, calls=%fused_computation.69 | loop fusion | bytes 4194336 | tf_op jit(solution)/shard_map/dynamic-slice.7
  70.7 0.7 copy.122
  71.4 3.9 %collective-permute-start.10 = (bf16[512,256]{1,0:T(8,128)(2,1)}, bf16[512,256]{1,0:T(8,128)(2,1)}, u32[]{:S(2)}, u32[]{:S(2)}) collective-permute-start(bf16[512,256]{1,0:T(8,128)(2,1)} %bitcast.128), channel_id=1, source_target_pairs={{0,20},{4,16},{8,28},{12,24},{16,4},{20,0},{24,12},{28,8},{1,21},{... | collective-permute-start | bytes 786440 | tf_op jit(solution)/shard_map/ppermute | solution.py:390
  75.3 0.8 copy.121
  76.1 1.0 collective-permute-start.11
  77.1 3.0 collective-permute-start.12
  84.5 2.0 copy.103
  87.1 1.3 collective-permute-start.6
  88.5 0.8 copy-done.7
  89.2 21.1 %place.1 = (bf16[4096,256]{1,0:T(8,128)(2,1)}, bf16[4096,256]{1,0:T(8,128)(2,1)}) custom-call(s32[1,4096]{1,0:T(1,128)} %bitcast.176, bf16[16,4096]{1,0:T(8,128)(2,1)} %concatenate.85.dt_ref, bf16[1024,256]{1,0:T(8,128)(2,1)} %bitcast.153, bf16[1024,256]{1,0:T(8,128)(2,1)} %collective-permute-done.3.refs_1_, ...), custom_call_target="tpu_custom_call" | custom-call | flops 12884901888 | bytes 6553600 | tf_op jit(solution)/shard_map/place/pallas_call | solution.py:240
  110.4 1.4 collective-permute-start.8
  111.8 1.4 collective-permute-start.9
  113.2 26.2 %fore.1 = (bf16[4096,256]{1,0:T(8,128)(2,1)}, f32[4096,256]{1,0:T(8,128)}, bf16[4096,256]{1,0:T(8,128)(2,1)}, f32[16,128,256]{2,1,0:T(8,128)}) custom-call(f32[4096]{0:T(1024)} %bitcast.177, f32[1,4096]{1,0:T(1,128)} %bitcast.170, f32[4096,1]{1,0:T(8,128)} %bitcast.145, s32[1,4096]{1,0:T(1,128)} %bitcast.154, bf16[4096,256]{1,0:T(8,128)(2,1)} %bitcast.13.x_ref, ...), custom_call_target="tpu_custom_call" | custom-call | flops 12784238592 | bytes 16384000 | tf_op jit(solution)/shard_map/fore/pallas_call | solution.py:258
  140.5 30.8 %back.1 = (bf16[4096,256]{1,0:T(8,128)(2,1)}, f32[4096,128]{1,0:T(8,128)}, f32[4096,128]{1,0:T(8,128)}, f32[4096,128]{1,0:T(8,128)}) custom-call(s32[8]{0:T(128)} %iota_xor_fusion.slot_smem, f32[4096]{0:T(1024)} %bitcast.178, s32[1]{0:T(128)} %bitcast.43.side_smem, f32[1,4096]{1,0:T(1,128)} %bitcast.171, f32[4096,1]{1,0:T(8,128)} %bitcast.146, ...), custom_call_target="tpu_custom_call" | custom-call | flops 8388608000 | bytes 24576000 | tf_op jit(solution)/shard_map/back/pallas_call | solution.py:287
  171.4 12.8 %gather_back.1 = bf16[4096,256]{1,0:T(8,128)(2,1)} custom-call(s32[4096,1]{1,0:T(8,128)} %copy.84.dest_col, bf16[4096,256]{1,0:T(8,128)(2,1)} %get-tuple-element.22.dx_ref), custom_call_target="tpu_custom_call" | custom-call | flops 8589934592 | bytes 6144000 | tf_op jit(solution)/shard_map/gather_back/pallas_call | solution.py:356
  184.2 4.5 %all-to-all-start.2 = ((bf16[8,512,256]{2,1,0:T(8,128)(2,1)}), bf16[8,512,256]{2,1,0:T(8,128)(2,1)}, u32[]{:S(2)}, u32[]{:S(2)}) async-start(bf16[8,512,256]{2,1,0:T(8,128)(2,1)} %bitcast.147), calls=%async_computation.2 | async-start | bytes 4194304 | tf_op jit(solution)/shard_map/all_to_all | solution.py:387
  189.5 3.7 %collective-permute-done.13.more_ref = f32[4096,128]{1,0:T(8,128)S(1)} collective-permute-done((f32[4096,128]{1,0:T(8,128)}, f32[4096,128]{1,0:T(8,128)S(1)}, u32[]{:S(2)}, u32[]{:S(2)}) %collective-permute-start.13) | collective-permute-done | bytes 2097184 | tf_op jit(solution)/shard_map/ppermute | solution.py:393
  193.2 1.4 copy-done.2
  194.5 5.4 %gather_rows.3 = f32[2048,128]{1,0:T(8,128)} custom-call(s32[2048]{0:T(1024)} %bitcast.173, f32[4096,128]{1,0:T(8,128)} %get-tuple-element.23.keep_ref, f32[4096,128]{1,0:T(8,128)} %copy-done.2), custom_call_target="tpu_custom_call" | custom-call | flops 524288 | bytes 6291456 | tf_op jit(solution)/shard_map/gather_rows/pallas_call | solution.py:321
  200.4 36.1 %all-to-all-done.2 = bf16[8,512,256]{2,1,0:T(8,128)(2,1)} async-done(((bf16[8,512,256]{2,1,0:T(8,128)(2,1)}), bf16[8,512,256]{2,1,0:T(8,128)(2,1)}, u32[]{:S(2)}, u32[]{:S(2)}) %all-to-all-start.2) | async-done | bytes 2097184 | tf_op jit(solution)/shard_map/all_to_all | solution.py:387
  236.6 3.6 %all-to-all-start.1 = ((bf16[8,512,256]{2,1,0:T(8,128)(2,1)}), bf16[8,512,256]{2,1,0:T(8,128)(2,1)S(1)}, u32[]{:S(2)}, u32[]{:S(2)}) async-start(bf16[8,512,256]{2,1,0:T(8,128)(2,1)} %bitcast.144), calls=%async_computation.1 | async-start | bytes 4194304 | tf_op jit(solution)/shard_map/all_to_all | solution.py:387
  240.2 5.4 %gather_rows.2 = f32[2048,128]{1,0:T(8,128)} custom-call(s32[2048]{0:T(1024)} %bitcast.172, f32[4096,128]{1,0:T(8,128)} %get-tuple-element.23.keep_ref, f32[4096,128]{1,0:T(8,128)} %copy-done.2), custom_call_target="tpu_custom_call" | custom-call | flops 524288 | bytes 6291456 | tf_op jit(solution)/shard_map/gather_rows/pallas_call | solution.py:321
  245.6 1.6 add.180
  247.2 0.8 dynamic-slice_bitcast_fusion
  248.1 2.0 collective-permute-start.15
  250.1 9.3 %gather_turn.1 = f32[8,4096]{1,0:T(8,128)} custom-call(s32[4096]{0:T(1024)} %dest_smem.1, f32[4096,128]{1,0:T(8,128)} %get-tuple-element.25.ddt_ref), custom_call_target="tpu_custom_call" | custom-call | flops 1048576 | bytes 4096000 | tf_op jit(solution)/shard_map/gather_turn/pallas_call | solution.py:338
  259.4 0.9 slice.37
  260.4 2.4 collective-permute-start.20
  262.8 14.1 %collective-permute-done.15 = f32[2,2,256,128]{3,2,1,0:T(8,128)} collective-permute-done((f32[2,2,256,128]{3,2,1,0:T(8,128)}, f32[2,2,256,128]{3,2,1,0:T(8,128)}, u32[]{:S(2)}, u32[]{:S(2)}) %collective-permute-start.15) | collective-permute-done | bytes 524320 | tf_op jit(solution)/shard_map/ppermute | solution.py:463
  277.0 1.1 bitcast_add_fusion
  278.2 11.2 %collective-permute-done.20 = bf16[1,2,2,4,512]{4,3,2,1,0:T(4,128)(2,1)S(1)} collective-permute-done((bf16[1,2,2,4,512]{4,3,2,1,0:T(4,128)(2,1)S(1)}, bf16[1,2,2,4,512]{4,3,2,1,0:T(4,128)(2,1)S(1)}, u32[]{:S(2)}, u32[]{:S(2)}) %collective-permute-start.20) | collective-permute-done | bytes 16416 | tf_op jit(solution)/shard_map/ppermute | solution.py:463
  289.6 5.5 %collective-permute-done.16 = f32[2,256,128]{2,1,0:T(8,128)S(1)} collective-permute-done((f32[2,256,128]{2,1,0:T(8,128)S(1)}, f32[2,256,128]{2,1,0:T(8,128)S(1)}, u32[]{:S(2)}, u32[]{:S(2)}) %collective-permute-start.16) | collective-permute-done | bytes 262176 | tf_op jit(solution)/shard_map/ppermute | solution.py:463
  295.5 8.3 %collective-permute-done.17 = f32[256,128]{1,0:T(8,128)S(1)} collective-permute-done((f32[256,128]{1,0:T(8,128)S(1)}, f32[256,128]{1,0:T(8,128)S(1)}, u32[]{:S(2)}, u32[]{:S(2)}) %collective-permute-start.17) | collective-permute-done | bytes 131104 | tf_op jit(solution)/shard_map/ppermute | solution.py:463
  304.0 1.1 collective-permute-done.18
  305.8 2.0 collective-permute-done.22
  308.4 3.2 %copy.99 = bf16[8,64,8,256]{3,2,0,1:T(8,128)(2,1)} copy(bf16[8,64,8,256]{3,2,1,0:T(8,128)(2,1)} %bitcast.72) | data formatting | bytes 4194304 | tf_op jit(solution)/shard_map/reshape | solution.py:401
  311.6 1.6 copy.98
  (127 shorter events, 16.6 us)
Async XLA Ops:
  0.6 1.5 copy-start
  2.4 14.0 %collective-permute-start = (bf16[1,208,256]{2,1,0:T(8,128)(2,1)S(1)}, bf16[1,208,256]{2,1,0:T(8,128)(2,1)S(1)}, u32[]{:S(2)}, u32[]{:S(2)}) collective-permute-start(bf16[1,208,256]{2,1,0:T(8,128)(2,1)S(1)} %maximum_bitcast_fusion), channel_id=1, source_target_pairs={{0,16},{4,20},{8,24},{12,28},{16,0},{20,4},{24,8},{28,12},{1,17},{... | collective-permute-start | bytes 319496 | tf_op jit(solution)/shard_map/ppermute | solution.py:390
  9.6 5.5 %copy-start.4 = (s32[4096]{0:T(1024)S(1)}, s32[4096]{0:T(1024)}, u32[]{:S(2)}) copy-start(s32[4096]{0:T(1024)} %dest_smem.1) | copy-start | bytes 49156
  9.6 103.7 %all-to-all-start = ((bf16[8,512,256]{2,1,0:T(8,128)(2,1)}), bf16[8,512,256]{2,1,0:T(8,128)(2,1)}, u32[]{:S(2)}, u32[]{:S(2)}) async-start(bf16[8,512,256]{2,1,0:T(8,128)(2,1)} %bitcast.125), calls=%async_computation | async-start | bytes 4194304 | tf_op jit(solution)/shard_map/all_to_all | solution.py:387
  16.4 37.1 %collective-permute-start.1 = (bf16[2,208,256]{2,1,0:T(8,128)(2,1)S(1)}, bf16[2,208,256]{2,1,0:T(8,128)(2,1)S(1)}, u32[]{:S(2)}, u32[]{:S(2)}) collective-permute-start(bf16[2,208,256]{2,1,0:T(8,128)(2,1)S(1)} %pad_maximum_fusion.6), channel_id=1, source_target_pairs={{0,8},{4,12},{8,0},{12,4},{16,24},{20,28},{24,16},{28,20},{1,9},{5... | collective-permute-start | bytes 638984 | tf_op jit(solution)/shard_map/ppermute | solution.py:390
  18.4 2.9 copy-start.12
  53.6 11.1 %collective-permute-start.2 = (bf16[4,208,256]{2,1,0:T(8,128)(2,1)S(1)}, bf16[4,208,256]{2,1,0:T(8,128)(2,1)S(1)}, u32[]{:S(2)}, u32[]{:S(2)}) collective-permute-start(bf16[4,208,256]{2,1,0:T(8,128)(2,1)S(1)} %pad_maximum_fusion.3), channel_id=1, source_target_pairs={{0,4},{4,0},{8,12},{12,8},{16,20},{20,16},{24,28},{28,24},{1,5},{5... | collective-permute-start | bytes 1277960 | tf_op jit(solution)/shard_map/ppermute | solution.py:390
  64.7 16.3 %copy-start.3 = (bf16[8,128,256]{2,1,0:T(8,128)(2,1)}, bf16[8,128,256]{2,1,0:T(8,128)(2,1)S(1)}, u32[]{:S(2)}) copy-start(bf16[8,128,256]{2,1,0:T(8,128)(2,1)S(1)} %pad_maximum_fusion) | copy-start | bytes 1572868
  64.7 17.7 %collective-permute-start.3 = (bf16[1024,256]{1,0:T(8,128)(2,1)S(1)}, bf16[1024,256]{1,0:T(8,128)(2,1)}, u32[]{:S(2)}, u32[]{:S(2)}) collective-permute-start(bf16[1024,256]{1,0:T(8,128)(2,1)S(1)} %bitcast.151), channel_id=1, source_target_pairs={{0,2},{1,3},{2,0},{3,1},{4,6},{5,7},{6,4},{7,5},{8,10},{9,11},{10,... | collective-permute-start | bytes 1572872 | tf_op jit(solution)/shard_map/ppermute | solution.py:393
  71.4 38.9 %collective-permute-start.10 = (bf16[512,256]{1,0:T(8,128)(2,1)}, bf16[512,256]{1,0:T(8,128)(2,1)}, u32[]{:S(2)}, u32[]{:S(2)}) collective-permute-start(bf16[512,256]{1,0:T(8,128)(2,1)} %bitcast.128), channel_id=1, source_target_pairs={{0,20},{4,16},{8,28},{12,24},{16,4},{20,0},{24,12},{28,8},{1,21},{... | collective-permute-start | bytes 786440 | tf_op jit(solution)/shard_map/ppermute | solution.py:390
  76.1 35.7 %collective-permute-start.11 = (bf16[512,256]{1,0:T(8,128)(2,1)}, bf16[512,256]{1,0:T(8,128)(2,1)}, u32[]{:S(2)}, u32[]{:S(2)}) collective-permute-start(bf16[512,256]{1,0:T(8,128)(2,1)} %bitcast.127), channel_id=1, source_target_pairs={{0,24},{4,28},{8,16},{12,20},{16,8},{20,12},{24,0},{28,4},{1,25},{... | collective-permute-start | bytes 786440 | tf_op jit(solution)/shard_map/ppermute | solution.py:390
  77.1 62.3 %collective-permute-start.12 = (bf16[512,256]{1,0:T(8,128)(2,1)S(1)}, bf16[512,256]{1,0:T(8,128)(2,1)}, u32[]{:S(2)}, u32[]{:S(2)}) collective-permute-start(bf16[512,256]{1,0:T(8,128)(2,1)S(1)} %bitcast.160), channel_id=1, source_target_pairs={{0,28},{4,24},{8,20},{12,16},{16,12},{20,8},{24,4},{28,0},{1,29},{... | collective-permute-start | bytes 786440 | tf_op jit(solution)/shard_map/ppermute | solution.py:390
  81.1 6.0 %collective-permute-start.4 = (bf16[1024,256]{1,0:T(8,128)(2,1)S(1)}, bf16[1024,256]{1,0:T(8,128)(2,1)}, u32[]{:S(2)}, u32[]{:S(2)}) collective-permute-start(bf16[1024,256]{1,0:T(8,128)(2,1)S(1)} %bitcast.152), channel_id=1, source_target_pairs={{0,1},{1,0},{2,3},{3,2},{4,5},{5,4},{6,7},{7,6},{8,9},{9,8},{10,11... | collective-permute-start | bytes 1572872 | tf_op jit(solution)/shard_map/ppermute | solution.py:393
  82.4 6.0 %collective-permute-start.5 = (bf16[1024,256]{1,0:T(8,128)(2,1)}, bf16[1024,256]{1,0:T(8,128)(2,1)S(1)}, u32[]{:S(2)}, u32[]{:S(2)}) collective-permute-start(bf16[1024,256]{1,0:T(8,128)(2,1)} %collective-permute-done.3.refs_1_), channel_id=1, source_target_pairs={{0,1},{1,0},{2,3},{3,2},{4,5},{5,4},{6,7},{7,6},{8,9},{9,8},{10,11... | collective-permute-start | bytes 1572872 | tf_op jit(solution)/shard_map/ppermute | solution.py:393
  84.5 25.9 %copy-start.6 = (f32[1,1,8,512]{3,1,2,0:T(1,128)}, f32[1,1,8,512]{3,1,2,0:T(1,128)S(1)}, u32[]{:S(2)}) copy-start(f32[1,1,8,512]{3,1,2,0:T(1,128)S(1)} %copy.101) | copy-start | bytes 49156
  87.1 52.3 %collective-permute-start.6 = (bf16[512,256]{1,0:T(8,128)(2,1)S(1)}, bf16[512,256]{1,0:T(8,128)(2,1)S(1)}, u32[]{:S(2)}, u32[]{:S(2)}) collective-permute-start(bf16[512,256]{1,0:T(8,128)(2,1)S(1)} %bitcast.162), channel_id=1, source_target_pairs={{0,4},{4,0},{8,12},{12,8},{16,20},{20,16},{24,28},{28,24},{1,5},{5... | collective-permute-start | bytes 786440 | tf_op jit(solution)/shard_map/ppermute | solution.py:390
  88.4 0.8 copy-start.7
  88.4 51.0 %collective-permute-start.7 = (bf16[512,256]{1,0:T(8,128)(2,1)S(1)}, bf16[512,256]{1,0:T(8,128)(2,1)S(1)}, u32[]{:S(2)}, u32[]{:S(2)}) collective-permute-start(bf16[512,256]{1,0:T(8,128)(2,1)S(1)} %bitcast.161), channel_id=1, source_target_pairs={{0,8},{4,12},{8,0},{12,4},{16,24},{20,28},{24,16},{28,20},{1,9},{5... | collective-permute-start | bytes 786440 | tf_op jit(solution)/shard_map/ppermute | solution.py:390
  110.4 29.1 %collective-permute-start.8 = (bf16[512,256]{1,0:T(8,128)(2,1)S(1)}, bf16[512,256]{1,0:T(8,128)(2,1)S(1)}, u32[]{:S(2)}, u32[]{:S(2)}) collective-permute-start(bf16[512,256]{1,0:T(8,128)(2,1)S(1)} %bitcast.159), channel_id=1, source_target_pairs={{0,12},{4,8},{8,4},{12,0},{16,28},{20,24},{24,20},{28,16},{1,13},{... | collective-permute-start | bytes 786440 | tf_op jit(solution)/shard_map/ppermute | solution.py:390
  111.8 27.7 %collective-permute-start.9 = (bf16[512,256]{1,0:T(8,128)(2,1)S(1)}, bf16[512,256]{1,0:T(8,128)(2,1)S(1)}, u32[]{:S(2)}, u32[]{:S(2)}) collective-permute-start(bf16[512,256]{1,0:T(8,128)(2,1)S(1)} %bitcast.158), channel_id=1, source_target_pairs={{0,16},{4,20},{8,24},{12,28},{16,0},{20,4},{24,8},{28,12},{1,17},{... | collective-permute-start | bytes 786440 | tf_op jit(solution)/shard_map/ppermute | solution.py:390
  139.4 0.7 copy-start.8
  139.5 0.8 copy-start.9
  139.5 0.9 copy-start.10
  139.5 1.0 copy-start.11
  184.2 4.6 %copy-start.5 = (s32[4096]{0:T(1024)S(1)}, s32[4096]{0:T(1024)}, u32[]{:S(2)}) copy-start(s32[4096]{0:T(1024)} %dest_smem.1) | copy-start | bytes 49156
  184.2 52.4 %all-to-all-start.2 = ((bf16[8,512,256]{2,1,0:T(8,128)(2,1)}), bf16[8,512,256]{2,1,0:T(8,128)(2,1)}, u32[]{:S(2)}, u32[]{:S(2)}) async-start(bf16[8,512,256]{2,1,0:T(8,128)(2,1)} %bitcast.147), calls=%async_computation.2 | async-start | bytes 4194304 | tf_op jit(solution)/shard_map/all_to_all | solution.py:387
  188.7 4.4 %collective-permute-start.13 = (f32[4096,128]{1,0:T(8,128)}, f32[4096,128]{1,0:T(8,128)S(1)}, u32[]{:S(2)}, u32[]{:S(2)}) collective-permute-start(f32[4096,128]{1,0:T(8,128)} %get-tuple-element.24), channel_id=1, source_target_pairs={{0,1},{1,0},{2,3},{3,2},{4,5},{5,4},{6,7},{7,6},{8,9},{9,8},{10,11... | collective-permute-start | bytes 6291464 | tf_op jit(solution)/shard_map/ppermute | solution.py:393
  193.2 1.4 copy-start.2
  199.9 45.6 %collective-permute-start.14 = (f32[2048,128]{1,0:T(8,128)}, f32[2048,128]{1,0:T(8,128)}, u32[]{:S(2)}, u32[]{:S(2)}) collective-permute-start(f32[2048,128]{1,0:T(8,128)} %gather_rows.3), channel_id=1, source_target_pairs={{0,2},{1,3},{2,0},{3,1},{4,6},{5,7},{6,4},{7,5},{8,10},{9,11},{10,... | collective-permute-start | bytes 3145736 | tf_op jit(solution)/shard_map/ppermute | solution.py:463
  236.6 75.1 %all-to-all-start.1 = ((bf16[8,512,256]{2,1,0:T(8,128)(2,1)}), bf16[8,512,256]{2,1,0:T(8,128)(2,1)S(1)}, u32[]{:S(2)}, u32[]{:S(2)}) async-start(bf16[8,512,256]{2,1,0:T(8,128)(2,1)} %bitcast.144), calls=%async_computation.1 | async-start | bytes 4194304 | tf_op jit(solution)/shard_map/all_to_all | solution.py:387
  248.1 28.9 %collective-permute-start.15 = (f32[2,2,256,128]{3,2,1,0:T(8,128)}, f32[2,2,256,128]{3,2,1,0:T(8,128)}, u32[]{:S(2)}, u32[]{:S(2)}) collective-permute-start(f32[2,2,256,128]{3,2,1,0:T(8,128)} %dynamic-slice_bitcast_fusion), channel_id=1, source_target_pairs={{0,4},{4,0},{8,12},{12,8},{16,20},{20,16},{24,28},{28,24},{1,5},{5... | collective-permute-start | bytes 1572872 | tf_op jit(solution)/shard_map/ppermute | solution.py:463
  260.4 29.0 %collective-permute-start.20 = (bf16[1,2,2,4,512]{4,3,2,1,0:T(4,128)(2,1)S(1)}, bf16[1,2,2,4,512]{4,3,2,1,0:T(4,128)(2,1)S(1)}, u32[]{:S(2)}, u32[]{:S(2)}) collective-permute-start(bf16[1,2,2,4,512]{4,3,2,1,0:T(4,128)(2,1)S(1)} %constant_dynamic-slice_fusion), channel_id=1, source_target_pairs={{0,16},{4,20},{8,24},{12,28},{16,0},{20,4},{24,8},{28,12},{1,17},{... | collective-permute-start | bytes 49160 | tf_op jit(solution)/shard_map/ppermute | solution.py:463
  278.1 16.9 %collective-permute-start.16 = (f32[2,256,128]{2,1,0:T(8,128)S(1)}, f32[2,256,128]{2,1,0:T(8,128)S(1)}, u32[]{:S(2)}, u32[]{:S(2)}) collective-permute-start(f32[2,256,128]{2,1,0:T(8,128)S(1)} %dynamic-slice_bitcast_fusion.1), channel_id=1, source_target_pairs={{0,8},{4,12},{8,0},{12,4},{16,24},{20,28},{24,16},{28,20},{1,9},{5... | collective-permute-start | bytes 786440 | tf_op jit(solution)/shard_map/ppermute | solution.py:463
  289.5 6.0 %collective-permute-start.21 = (bf16[2,1,2,4,512]{4,3,2,1,0:T(4,128)(2,1)S(1)}, bf16[2,1,2,4,512]{4,3,2,1,0:T(4,128)(2,1)S(1)}, u32[]{:S(2)}, u32[]{:S(2)}) collective-permute-start(bf16[2,1,2,4,512]{4,3,2,1,0:T(4,128)(2,1)S(1)} %fusion.3), channel_id=1, source_target_pairs={{0,8},{4,12},{8,0},{12,4},{16,24},{20,28},{24,16},{28,20},{1,9},{5... | collective-permute-start | bytes 49160 | tf_op jit(solution)/shard_map/ppermute | solution.py:463
  295.1 8.7 %collective-permute-start.17 = (f32[256,128]{1,0:T(8,128)S(1)}, f32[256,128]{1,0:T(8,128)S(1)}, u32[]{:S(2)}, u32[]{:S(2)}) collective-permute-start(f32[256,128]{1,0:T(8,128)S(1)} %dynamic-slice_bitcast_fusion.2), channel_id=1, source_target_pairs={{0,16},{4,20},{8,24},{12,28},{16,0},{20,4},{24,8},{28,12},{1,17},{... | collective-permute-start | bytes 393224 | tf_op jit(solution)/shard_map/ppermute | solution.py:463
  303.8 1.3 collective-permute-start.18
  304.0 3.8 %collective-permute-start.22 = (bf16[2,2,1,4,512]{4,3,2,1,0:T(4,128)(2,1)S(1)}, bf16[2,2,1,4,512]{4,3,2,1,0:T(4,128)(2,1)S(1)}, u32[]{:S(2)}, u32[]{:S(2)}) collective-permute-start(bf16[2,2,1,4,512]{4,3,2,1,0:T(4,128)(2,1)S(1)} %fusion.1), channel_id=1, source_target_pairs={{0,4},{4,0},{8,12},{12,8},{16,20},{20,16},{24,28},{28,24},{1,5},{5... | collective-permute-start | bytes 49160 | tf_op jit(solution)/shard_map/ppermute | solution.py:463
  305.2 8.0 %collective-permute-start.19 = (bf16[256,256]{1,0:T(8,128)(2,1)S(1)}, bf16[256,256]{1,0:T(8,128)(2,1)S(1)}, u32[]{:S(2)}, u32[]{:S(2)}) collective-permute-start(bf16[256,256]{1,0:T(8,128)(2,1)S(1)} %pad_maximum_fusion.7), channel_id=1, source_target_pairs={{0,2},{1,3},{2,0},{3,1},{4,6},{5,7},{6,4},{7,5},{8,10},{9,11},{10,... | collective-permute-start | bytes 393224 | tf_op jit(solution)/shard_map/ppermute | solution.py:393
  311.6 2.4 copy-start.1
